TPU v7x, 256 devices: a whole 4x4x8 slice. The times are simulated.
256 devices in a mesh: group: 16 (over x, y_hi, core), member: 16 (over y_lo, z).
Axes of the slice: x: 4, y: 4 (y_hi: 2, y_lo: 2; y = y_hi * 2 + y_lo), z: 8, core: 2. Of those that a mesh axis runs over, the one named last changes fastest.
Arguments:
- spectra: bfloat16 [8192, 8, 2048], P(('group', 'member'))
- partner: int32 [16], replicated, may hold values from 0 to 15, as said below
Outputs:
- correlations: bfloat16 [8192, 512, 128], P(('group', 'member'))
Inputs may be any that keep to these rules, and one draw needn't show every extreme that they name: partner is one round of a round-robin among the 16 groups: partner[partner[g]] == g and partner[g] != g for every g.
All inputs are finite; a program needn't handle non-finite values.
Results may differ from a plain program's by a relative error of at most 0.007.
Values may be sent and summed in bfloat16 or wider, within the bound.
A program may use at most 192 MiB of HBM per device.

v0:
```python
import math

import jax
import jax.numpy as jnp
from jax import lax
from jax.sharding import PartitionSpec as P

LAGS = 128
HALF = 64


def band_matrix(freq_count):
    positions = jnp.arange(freq_count, dtype=jnp.int32)
    distance = jnp.abs(positions[:, None] - positions[None, :])
    band_ones = (distance <= HALF).astype(jnp.float32)
    counts = (
        jnp.minimum(positions + HALF, freq_count - 1) - jnp.maximum(positions - HALF, 0) + 1
    ).astype(jnp.float32)
    return (band_ones, counts)


def whiten(spectra):
    freq_count = spectra.shape[2] // 2
    window_count = spectra.shape[1]
    real_part = spectra[:, :, :freq_count].astype(jnp.float32)
    imag_part = spectra[:, :, freq_count:].astype(jnp.float32)
    power_sum = jnp.sum(real_part * real_part + imag_part * imag_part, axis=1)
    band_ones, counts = band_matrix(freq_count)
    smoothed = jnp.dot(power_sum, band_ones, precision=lax.Precision.HIGHEST)
    average = smoothed / (counts * window_count)
    inverse_amp = 1.0 / jnp.sqrt(average + 1e-05)
    factor = jnp.concatenate([inverse_amp, inverse_amp], axis=1)
    return (spectra.astype(jnp.float32) * factor[:, None, :]).astype(jnp.bfloat16)


def lag_matrix(freq_count, window_count):
    lag_values = jnp.arange(LAGS, dtype=jnp.int32) - LAGS // 2
    freq_values = jnp.arange(freq_count, dtype=jnp.int32)
    residue = jnp.mod(freq_values[:, None] * lag_values[None, :], 2 * freq_count)
    angles = jnp.pi * residue.astype(jnp.float32) / freq_count
    norm_factor = 1.0 / math.sqrt(window_count * freq_count)
    return jnp.concatenate(
        [jnp.cos(angles) * norm_factor, -jnp.sin(angles) * norm_factor], axis=0
    ).astype(jnp.bfloat16)


def correlate(own_rows, other_rows, lag_table):
    freq_count = own_rows.shape[2] // 2
    own_real = own_rows[:, :, :freq_count]
    own_imag = own_rows[:, :, freq_count:]
    left_real = jnp.concatenate([own_real, own_imag], axis=1)
    left_imag = jnp.concatenate([own_imag, -own_real], axis=1)
    right_part = jnp.concatenate(
        [other_rows[:, :, :freq_count], other_rows[:, :, freq_count:]], axis=1
    )
    cross_real = jnp.einsum(
        "awf,bwf->abf", left_real, right_part, preferred_element_type=jnp.float32
    )
    cross_imag = jnp.einsum(
        "awf,bwf->abf", left_imag, right_part, preferred_element_type=jnp.float32
    )
    cross = jnp.concatenate([cross_real, cross_imag], axis=2).astype(jnp.bfloat16)
    own_count = own_rows.shape[0]
    other_count = other_rows.shape[0]
    lagged = jnp.dot(
        cross.reshape(own_count * other_count, 2 * freq_count),
        lag_table,
        preferred_element_type=jnp.float32,
    )
    return lagged.reshape(own_count, other_count, lag_table.shape[1])


def correlate_blocks(own_rows, other_rows, lag_table):
    row_count = other_rows.shape[0]
    block_size = math.gcd(row_count, max(1, 2048 // own_rows.shape[0]))
    stacked = other_rows.reshape((row_count // block_size, block_size) + other_rows.shape[1:])
    blocks_out = lax.map(lambda portion: correlate(own_rows, portion, lag_table), stacked)
    return jnp.transpose(blocks_out, (1, 0, 2, 3)).reshape(
        own_rows.shape[0], row_count, lag_table.shape[1]
    )


def on_device(spectra, partner):
    whitened = whiten(spectra)
    group_count = lax.axis_size("group")
    row_count = whitened.shape[0]
    spread = lax.all_to_all(whitened, "group", split_axis=0, concat_axis=0, tiled=True)
    blocks = spread.reshape((group_count, row_count // group_count) + whitened.shape[1:])
    ordered = jnp.take(blocks, partner, axis=0).reshape(whitened.shape)
    arrived = lax.all_to_all(ordered, "group", split_axis=0, concat_axis=0, tiled=True)
    lag_table = lag_matrix(whitened.shape[2] // 2, whitened.shape[1])
    member_count = lax.axis_size("member")
    side = math.isqrt(member_count)
    piece = row_count // side
    tail = whitened.shape[1:]
    own_send = jnp.repeat(whitened.reshape((side, piece) + tail), side, axis=0).reshape(
        (member_count * piece,) + tail
    )
    other_send = jnp.tile(arrived.reshape((side, piece) + tail), (side, 1, 1, 1)).reshape(
        (member_count * piece,) + tail
    )
    own_tile, other_tile = (
        lax.all_to_all(own_send, "member", split_axis=0, concat_axis=0, tiled=True),
        lax.all_to_all(other_send, "member", split_axis=0, concat_axis=0, tiled=True),
    )
    tile_out = correlate_blocks(own_tile, other_tile, lag_table).astype(jnp.bfloat16)
    lag_count = lag_table.shape[1]
    back_send = tile_out.reshape(member_count, piece, member_count * piece, lag_count)
    returned = lax.all_to_all(back_send, "member", split_axis=0, concat_axis=0, tiled=True)
    arranged = returned.reshape(side, side, piece, member_count, piece, lag_count)
    arranged = jnp.transpose(arranged, (0, 2, 3, 1, 4, 5))
    result = arranged.reshape(row_count, member_count * row_count, lag_count)
    return result


def solution(mesh):
    placed = (P(("group", "member"), None, None), P())
    return jax.shard_map(
        on_device,
        mesh=mesh,
        in_specs=placed,
        out_specs=P(("group", "member"), None, None),
        check_vma=False,
    )
```

profile of v0, /device:TPU:1, one launch (start us, length us, event | category | flops | bytes accessed | tf_op | source)
XLA Modules:
  0.0 630.5 jit_solution(10255185979265269614)
XLA Ops:
  0.0 1.7 add_reduce_fusion
  2.5 1.2 multiply_convert_fusion
  3.8 8.4 %all-to-all-start = ((bf16[32,8,2048]{2,1,0:T(8,128)(2,1)}), bf16[32,8,2048]{2,1,0:T(8,128)(2,1)S(1)}, u32[]{:S(2)}, u32[]{:S(2)}) async-start(bf16[32,8,2048]{2,1,0:T(8,128)(2,1)} %multiply_convert_fusion), calls=%async_computation | async-start | bytes 2097152 | tf_op jit(solution)/shard_map/all_to_all | solution.py:87
  12.4 16.7 %all-to-all-done = bf16[32,8,2048]{2,1,0:T(8,128)(2,1)S(1)} async-done(((bf16[32,8,2048]{2,1,0:T(8,128)(2,1)}), bf16[32,8,2048]{2,1,0:T(8,128)(2,1)S(1)}, u32[]{:S(2)}, u32[]{:S(2)}) %all-to-all-start) | async-done | bytes 1048608 | tf_op jit(solution)/shard_map/all_to_all | solution.py:87
  30.0 20.7 %all_to_all.25 = bf16[32,8,2048]{2,1,0:T(8,128)(2,1)S(1)} all-to-all(bf16[32,8,2048]{2,1,0:T(8,128)(2,1)S(1)} %bitcast_select_fusion), channel_id=1, replica_groups=mesh['group'=16,'member'=16] {'group'}, dimensions={0} | all-to-all | bytes 2097152 | tf_op jit(solution)/shard_map/all_to_all | solution.py:90
  50.7 1.7 broadcast_in_dim.36
  52.5 99.9 %all_to_all.26 = bf16[128,8,2048]{2,1,0:T(8,128)(2,1)} all-to-all(bf16[128,8,2048]{2,1,0:T(8,128)(2,1)S(1)} %bitcast.53), channel_id=1, replica_groups=mesh['group'=16,'member'=16] {'member'}, dimensions={0} | all-to-all | bytes 8388608 | tf_op jit(solution)/shard_map/all_to_all | solution.py:103
  152.4 2.5 tile.10
  154.9 6.2 all-to-all-start.2
  161.0 2.2 multiply_convert_fusion.2
  163.3 2.6 slice_negate_fusion
  166.0 3.8 pad_maximum_fusion.3
  169.7 7.3 %copy.17 = bf16[128,16,1024]{0,1,2:T(8,128)(2,1)} copy(bf16[128,16,1024]{2,1,0:T(8,128)(2,1)} %get-tuple-element.103) | data formatting | bytes 8388608 | tf_op jit(solution)/shard_map/while | solution.py:77
  177.0 7.3 %copy.18 = bf16[128,16,1024]{0,1,2:T(8,128)(2,1)} copy(bf16[128,16,1024]{2,1,0:T(8,128)(2,1)} %get-tuple-element.102) | data formatting | bytes 8388608 | tf_op jit(solution)/shard_map/while | solution.py:77
  184.3 71.5 %all-to-all-done.2 = bf16[128,8,2048]{2,1,0:T(8,128)(2,1)} async-done(((bf16[128,8,2048]{2,1,0:T(8,128)(2,1)}), bf16[128,8,2048]{2,1,0:T(8,128)(2,1)}, u32[]{:S(2)}, u32[]{:S(2)}) %all-to-all-start.2) | async-done | bytes 4194336 | tf_op jit(solution)/shard_map/all_to_all | solution.py:104
  255.8 266.6 %while.12 = (s32[]{:T(128)}, bf16[8,128,16,128]{3,1,2,0:T(8,128)(2,1)}, bf16[8,16,8,2048]{3,2,1,0:T(8,128)(2,1)}, bf16[128,16,1024]{0,1,2:T(8,128)(2,1)}, bf16[1...) while((s32[]{:T(128)}, bf16[8,128,16,128]{3,1,2,0:T(8,128)(2,1)}, ...), condition=%wide.region_2.3_spmd, body=%wide.region_1.2_spmd.sunk | while | flops 1217396736 | bytes 67633800 | solution.py:77
  255.8 1.1 dynamic-slice_bitcast_fusion.2
  256.9 4.7 copy.30
  261.7 5.9 convert_bitcast_fusion.5
  267.6 2.3 convert_bitcast_fusion.6
  269.9 14.7 %pad_maximum_fusion.9 = bf16[128,16,2048]{0,1,2:T(8,128)(2,1)S(1)} fusion(bf16[128,16,1024]{0,1,2:T(8,128)(2,1)S(1)} %convert_bitcast_fusion.5, bf16[128,16,1024]{0,1,2:T(8,128)(2,1)S(1)} %convert_bitcast_fusion.6), kind=kLoop, calls=%fused_computation.1.clone.1 | loop fusion | flops 4194304 | bytes 16777216 | tf_op jit(solution)/shard_map/while/body/eval_jaxpr/concatenate | solution.py:62
  284.6 4.5 fusion.48
  289.1 1.1 dynamic-slice_bitcast_fusion.2
  290.3 4.7 copy.30
  295.0 5.9 convert_bitcast_fusion.5
  301.0 2.3 convert_bitcast_fusion.6
  303.3 14.7 %pad_maximum_fusion.9 = bf16[128,16,2048]{0,1,2:T(8,128)(2,1)S(1)} fusion(bf16[128,16,1024]{0,1,2:T(8,128)(2,1)S(1)} %convert_bitcast_fusion.5, bf16[128,16,1024]{0,1,2:T(8,128)(2,1)S(1)} %convert_bitcast_fusion.6), kind=kLoop, calls=%fused_computation.1.clone.1 | loop fusion | flops 4194304 | bytes 16777216 | tf_op jit(solution)/shard_map/while/body/eval_jaxpr/concatenate | solution.py:62
  318.0 4.5 fusion.48
  322.4 1.1 dynamic-slice_bitcast_fusion.2
  323.6 4.7 copy.30
  328.4 5.9 convert_bitcast_fusion.5
  334.3 2.3 convert_bitcast_fusion.6
  336.6 14.7 %pad_maximum_fusion.9 = bf16[128,16,2048]{0,1,2:T(8,128)(2,1)S(1)} fusion(bf16[128,16,1024]{0,1,2:T(8,128)(2,1)S(1)} %convert_bitcast_fusion.5, bf16[128,16,1024]{0,1,2:T(8,128)(2,1)S(1)} %convert_bitcast_fusion.6), kind=kLoop, calls=%fused_computation.1.clone.1 | loop fusion | flops 4194304 | bytes 16777216 | tf_op jit(solution)/shard_map/while/body/eval_jaxpr/concatenate | solution.py:62
  351.3 4.5 fusion.48
  355.8 1.1 dynamic-slice_bitcast_fusion.2
  356.9 4.7 copy.30
  361.7 5.9 convert_bitcast_fusion.5
  367.6 2.3 convert_bitcast_fusion.6
  369.9 14.7 %pad_maximum_fusion.9 = bf16[128,16,2048]{0,1,2:T(8,128)(2,1)S(1)} fusion(bf16[128,16,1024]{0,1,2:T(8,128)(2,1)S(1)} %convert_bitcast_fusion.5, bf16[128,16,1024]{0,1,2:T(8,128)(2,1)S(1)} %convert_bitcast_fusion.6), kind=kLoop, calls=%fused_computation.1.clone.1 | loop fusion | flops 4194304 | bytes 16777216 | tf_op jit(solution)/shard_map/while/body/eval_jaxpr/concatenate | solution.py:62
  384.6 4.5 fusion.48
  389.1 1.1 dynamic-slice_bitcast_fusion.2
  390.3 4.7 copy.30
  395.0 5.9 convert_bitcast_fusion.5
  401.0 2.3 convert_bitcast_fusion.6
  403.3 14.7 %pad_maximum_fusion.9 = bf16[128,16,2048]{0,1,2:T(8,128)(2,1)S(1)} fusion(bf16[128,16,1024]{0,1,2:T(8,128)(2,1)S(1)} %convert_bitcast_fusion.5, bf16[128,16,1024]{0,1,2:T(8,128)(2,1)S(1)} %convert_bitcast_fusion.6), kind=kLoop, calls=%fused_computation.1.clone.1 | loop fusion | flops 4194304 | bytes 16777216 | tf_op jit(solution)/shard_map/while/body/eval_jaxpr/concatenate | solution.py:62
  418.0 4.5 fusion.48
  423.6 4.7 copy.30
  428.3 5.9 convert_bitcast_fusion.5
  434.3 2.3 convert_bitcast_fusion.6
  436.6 14.7 %pad_maximum_fusion.9 = bf16[128,16,2048]{0,1,2:T(8,128)(2,1)S(1)} fusion(bf16[128,16,1024]{0,1,2:T(8,128)(2,1)S(1)} %convert_bitcast_fusion.5, bf16[128,16,1024]{0,1,2:T(8,128)(2,1)S(1)} %convert_bitcast_fusion.6), kind=kLoop, calls=%fused_computation.1.clone.1 | loop fusion | flops 4194304 | bytes 16777216 | tf_op jit(solution)/shard_map/while/body/eval_jaxpr/concatenate | solution.py:62
  451.3 4.5 fusion.48
  456.9 4.7 copy.30
  461.7 5.9 convert_bitcast_fusion.5
  467.6 2.3 convert_bitcast_fusion.6
  469.9 14.7 %pad_maximum_fusion.9 = bf16[128,16,2048]{0,1,2:T(8,128)(2,1)S(1)} fusion(bf16[128,16,1024]{0,1,2:T(8,128)(2,1)S(1)} %convert_bitcast_fusion.5, bf16[128,16,1024]{0,1,2:T(8,128)(2,1)S(1)} %convert_bitcast_fusion.6), kind=kLoop, calls=%fused_computation.1.clone.1 | loop fusion | flops 4194304 | bytes 16777216 | tf_op jit(solution)/shard_map/while/body/eval_jaxpr/concatenate | solution.py:62
  484.6 4.5 fusion.48
  490.3 4.7 copy.30
  495.0 5.9 convert_bitcast_fusion.5
  500.9 2.3 convert_bitcast_fusion.6
  503.3 14.7 %pad_maximum_fusion.9 = bf16[128,16,2048]{0,1,2:T(8,128)(2,1)S(1)} fusion(bf16[128,16,1024]{0,1,2:T(8,128)(2,1)S(1)} %convert_bitcast_fusion.5, bf16[128,16,1024]{0,1,2:T(8,128)(2,1)S(1)} %convert_bitcast_fusion.6), kind=kLoop, calls=%fused_computation.1.clone.1 | loop fusion | flops 4194304 | bytes 16777216 | tf_op jit(solution)/shard_map/while/body/eval_jaxpr/concatenate | solution.py:62
  517.9 4.5 fusion.48
  522.4 4.9 copy.19
  527.3 100.4 %all_to_all.27 = bf16[16,8,128,128]{3,2,1,0:T(8,128)(2,1)S(1)} all-to-all(bf16[16,8,128,128]{3,2,1,0:T(8,128)(2,1)S(1)} %bitcast.54), channel_id=1, replica_groups=mesh['group'=16,'member'=16] {'member'}, dimensions={0} | all-to-all | bytes 8388608 | tf_op jit(solution)/shard_map/all_to_all | solution.py:109
  627.7 2.8 copy.20
  (68 shorter events, 5.7 us)
Async XLA Ops:
  0.0 2.5 copy-start.2
  1.7 10.5 %copy-start.3 = (s32[16]{0:T(128)S(1)}, s32[16]{0:T(128)}, u32[]{:S(2)}) copy-start(s32[16]{0:T(128)} %param.5) | copy-start | bytes 196
  3.8 25.4 %all-to-all-start = ((bf16[32,8,2048]{2,1,0:T(8,128)(2,1)}), bf16[32,8,2048]{2,1,0:T(8,128)(2,1)S(1)}, u32[]{:S(2)}, u32[]{:S(2)}) async-start(bf16[32,8,2048]{2,1,0:T(8,128)(2,1)} %multiply_convert_fusion), calls=%async_computation | async-start | bytes 2097152 | tf_op jit(solution)/shard_map/all_to_all | solution.py:87
  154.9 100.9 %all-to-all-start.2 = ((bf16[128,8,2048]{2,1,0:T(8,128)(2,1)}), bf16[128,8,2048]{2,1,0:T(8,128)(2,1)}, u32[]{:S(2)}, u32[]{:S(2)}) async-start(bf16[128,8,2048]{2,1,0:T(8,128)(2,1)} %bitcast.52), calls=%async_computation.2 | async-start | bytes 8388608 | tf_op jit(solution)/shard_map/all_to_all | solution.py:104
  261.7 5.9 copy-start
  261.7 5.9 copy-start.1
  295.0 5.9 copy-start
  295.0 5.9 copy-start.1
  328.3 5.9 copy-start
  328.4 5.9 copy-start.1
  361.7 5.9 copy-start
  361.7 5.9 copy-start.1
  395.0 5.9 copy-start
  395.0 5.9 copy-start.1
  428.3 5.9 copy-start
  428.3 5.9 copy-start.1
  461.7 5.9 copy-start
  461.7 5.9 copy-start.1
  495.0 5.9 copy-start
  495.0 5.9 copy-start.1
where the time goes:
time: 633 us; the launch traced here: 631 us
  blocking collectives  221 us (35%)
  other arithmetic  130 us (21%)
  matrix products  102 us (16%)
  waiting for transfers between devices  88.2 us (14%)
  local copies, waits for them, and re-layouts  74.2 us (12%)
  starting transfers between devices  14.6 us (2%)
    concatenate x8, other arithmetic, correlate(): jnp.concatenate([cross_real, cross_imag], axis=2).astype(jnp.bfloat16)  117 us
    all_to_all x1, blocking collectives, on_device(): lax.all_to_all(back_send, 'member', split_axis=0, concat_axis=0, tiled=True)  100 us
    all_to_all x1, blocking collectives, on_device(): lax.all_to_all(own_send, 'member', split_axis=0, concat_axis=0, tiled=True)  99.9 us
    all_to_all x1, waiting for transfers between devices, on_device(): lax.all_to_all(other_send, 'member', split_axis=0, concat_axis=0, tiled=T...  71.5 us
    dot_general x8, matrix products, correlate(): jnp.einsum('awf,bwf->abf', left_imag, right_part, preferred_element_type=...  47.3 us
    concatenate x8, local copies, waits for them, and re-layouts, correlate(): jnp.concatenate([other_rows[:, :, :freq_count], other_rows[:, :, freq_cou...  38 us
    dot_general x8, matrix products, correlate(): jnp.dot(cross.reshape(own_count * other_count, 2 * freq_count), lag_table...  35.8 us
    all_to_all x1, blocking collectives, on_device(): lax.all_to_all(ordered, 'group', split_axis=0, concat_axis=0, tiled=True)  20.7 us
  transfers between devices with their start and end apart: 2, of which 2 were waited for; matrix products, arithmetic and copies ran while one was open for 4% of the time, Pallas kernels for 0%

commit v1 on v0

v1 whole, which is shorter than its diff:
```python
import functools
import math

import jax
import jax.numpy as jnp
from jax import lax
from jax.experimental import pallas as pl
from jax.experimental.pallas import tpu as pltpu
from jax.sharding import Mesh
from jax.sharding import PartitionSpec as P

LAGS = 128
HALF = 64
FREQS = 1024
WINDOWS = 8
CH = 32
COLS = 128
INNER = 8
CHUNK = 16
STEPS = COLS // CHUNK
TILE = 256
AXES = ("x", "yh", "core", "ylo", "z")
MESH = pl.DeviceIdType.MESH

SLOT = {0: 0, 1: 1, -1: 2, 2: 3, -2: 4, 3: 5, -3: 6, 4: 7}
DIST = {slot: dist for dist, slot in SLOT.items()}


def band_matrix():
    positions = jnp.arange(FREQS, dtype=jnp.int32)
    distance = jnp.abs(positions[:, None] - positions[None, :])
    band_ones = (distance <= HALF).astype(jnp.float32)
    counts = (
        jnp.minimum(positions + HALF, FREQS - 1) - jnp.maximum(positions - HALF, 0) + 1
    ).astype(jnp.float32)
    return band_ones, counts


def whiten(spectra):
    real_part = spectra[:, :, :FREQS].astype(jnp.float32)
    imag_part = spectra[:, :, FREQS:].astype(jnp.float32)
    power_sum = jnp.sum(real_part * real_part + imag_part * imag_part, axis=1)
    band_ones, counts = band_matrix()
    smoothed = jnp.dot(power_sum, band_ones, precision=lax.Precision.HIGHEST)
    average = smoothed / (counts * WINDOWS)
    inverse_amp = 1.0 / jnp.sqrt(average + 1e-05)
    factor = jnp.concatenate([inverse_amp, inverse_amp], axis=1)
    return (spectra.astype(jnp.float32) * factor[:, None, :]).astype(jnp.bfloat16)


def lag_rows():
    lag_values = jnp.arange(LAGS, dtype=jnp.int32) - LAGS // 2
    columns = jnp.arange(COLS, dtype=jnp.int32).reshape(STEPS, CHUNK)
    freq = columns[:, :, None] + COLS * jnp.arange(INNER, dtype=jnp.int32)[None, None, :]
    residue = jnp.mod(freq[:, None, :, :] * lag_values[None, :, None, None], 2 * FREQS)
    angles = jnp.pi * residue.astype(jnp.float32) / FREQS
    norm_factor = 1.0 / math.sqrt(WINDOWS * FREQS)
    table = jnp.stack([jnp.cos(angles) * norm_factor, -jnp.sin(angles) * norm_factor], axis=3)
    return table.reshape(STEPS, LAGS, CHUNK * 2 * INNER).astype(jnp.bfloat16)


def pair_kernel(
    own_ref, part_ref, lag_ref, out_ref,
    x_rows, xs_rows, gathered, left, cross, total, result,
    own_sem, recv_sem, send_sem, out_send, out_recv,
):
    core = lax.axis_index("core")
    ylo = lax.axis_index("ylo")
    z = lax.axis_index("z")
    up = lax.rem(z + 1, 8)
    down = lax.rem(z + 7, 8)
    moved = core != ylo

    barrier = pltpu.get_barrier_semaphore()
    pl.semaphore_signal(barrier, inc=1, device_id={"z": up}, device_id_type=MESH)
    pl.semaphore_signal(barrier, inc=1, device_id={"z": down}, device_id_type=MESH)
    pl.semaphore_signal(barrier, inc=1, device_id={"core": 1 - core}, device_id_type=MESH)

    @pl.when(moved)
    def _():
        pl.semaphore_signal(
            barrier, inc=1, device_id={"core": ylo, "ylo": core}, device_id_type=MESH
        )
        pl.semaphore_wait(barrier, 4)

    @pl.when(jnp.logical_not(moved))
    def _():
        pl.semaphore_wait(barrier, 3)

    def columns(c):
        return pl.ds(pl.multiple_of(c * CHUNK, CHUNK), CHUNK)

    def place(c, dist, member):
        start = SLOT[dist] * 64 + member * 32
        return gathered.at[columns(c), pl.ds(pl.multiple_of(start, 32), 32), :]

    def source(c, dist):
        return part_ref.at[columns(c)] if dist == 0 else place(c, dist, core)

    def hop(c, dist, step):
        landed = 4 if dist + step == -4 else dist + step
        return pltpu.make_async_remote_copy(
            src_ref=source(c, dist),
            dst_ref=place(c, landed, core),
            send_sem=send_sem.at[c, SLOT[landed] - 1],
            recv_sem=recv_sem.at[c, 0, SLOT[landed]],
            device_id={"z": down if step == 1 else up},
            device_id_type=MESH,
        )

    def across(c, dist):
        return pltpu.make_async_remote_copy(
            src_ref=source(c, dist),
            dst_ref=place(c, dist, core),
            send_sem=send_sem.at[c, 7 + SLOT[dist]],
            recv_sem=recv_sem.at[c, 1, SLOT[dist]],
            device_id={"core": 1 - core},
            device_id_type=MESH,
        )

    def own_copy(c):
        return pltpu.make_async_copy(part_ref.at[columns(c)], place(c, 0, core), own_sem.at[c])

    def result_pieces(tile):
        for piece in range(4):
            from_z = lax.rem(z + DIST[tile * 4 + piece] + 8, 8)
            for member in range(2):
                rows = pl.ds(piece * 64 + member * 32, 32)
                target = pl.ds(pl.multiple_of((member * 8 + from_z) * 32, 32), 32)
                yield tile * 8 + piece * 2 + member, result.at[tile, :, rows, :], target

    def result_remote(index, src, target):
        return pltpu.make_async_remote_copy(
            src_ref=src, dst_ref=out_ref.at[:, target, :],
            send_sem=out_send.at[index], recv_sem=out_recv.at[index],
            device_id={"core": ylo, "ylo": core}, device_id_type=MESH,
        )

    def result_local(index, src, target):
        return pltpu.make_async_copy(src, out_ref.at[:, target, :], out_send.at[index])

    def send_result(tile):
        @pl.when(moved)
        def _():
            for piece in result_pieces(tile):
                result_remote(*piece).start()

        @pl.when(jnp.logical_not(moved))
        def _():
            for piece in result_pieces(tile):
                result_local(*piece).start()

    lane = lax.broadcasted_iota(jnp.int32, (INNER, COLS), 1)
    row = lax.broadcasted_iota(jnp.int32, (INNER, COLS), 0)
    mask = lax.rem(lane // WINDOWS, INNER) == row
    sign = jnp.where(lax.broadcasted_iota(jnp.int32, (CH, COLS), 1) < 64, 1.0, -1.0)

    def load_rows(column):
        value = own_ref[column].astype(jnp.float32)
        x_rows[column] = value
        xs_rows[column] = pltpu.roll(value, 64, 1) * sign

    def cross_column(c, i, tile):
        column = c * CHUNK + i
        for a in range(CH):
            re_row = jnp.broadcast_to(x_rows[column, pl.ds(a, 1), :], (INNER, COLS))
            im_row = jnp.broadcast_to(xs_rows[column, pl.ds(a, 1), :], (INNER, COLS))
            block = jnp.concatenate(
                [jnp.where(mask, re_row, 0.0), jnp.where(mask, im_row, 0.0)], axis=0
            )
            left[pl.ds(a * 16, 16), :] = block.astype(jnp.bfloat16)
        right = gathered[column, pl.ds(pl.multiple_of(tile * TILE, TILE), TILE), :]
        product = lax.dot_general(
            left[...], right, (((1,), (1,)), ((), ())), preferred_element_type=jnp.float32
        )
        cross[:, pl.ds(pl.multiple_of(i * 16, 16), 16), :] = product.astype(
            jnp.bfloat16
        ).reshape(CH, 16, TILE)

    def lag_channel(c, a, first):
        product = jnp.dot(lag_ref[c], cross[a], preferred_element_type=jnp.float32)

        @pl.when(first)
        def _():
            total[a] = product

        @pl.when(jnp.logical_not(first))
        def _():
            total[a] = total[a] + product

    def compute(c, tile):
        @pl.loop(0, CHUNK)
        def _(i):
            cross_column(c, i, tile)

        @pl.loop(0, CH)
        def _(a):
            lag_channel(c, a, c == 0)

        @pl.when(c == STEPS - 1)
        def _():
            @pl.loop(0, CH)
            def _(a):
                result[tile, a] = total[a].T.astype(jnp.bfloat16)

    def inside(c):
        return jnp.logical_and(c >= 0, c < STEPS)

    @pl.loop(0, 2 * STEPS + 3)
    def _(tick):
        t = tick - 3

        @pl.when(inside(t + 3))
        def _():
            c = t + 3
            own_copy(c).start()
            hop(c, 0, 1).start()
            hop(c, 0, -1).start()
            across(c, 0).start()

        @pl.when(inside(t + 2))
        def _():
            c = t + 2
            hop(c, 0, 1).wait_recv()
            hop(c, 1, 1).start()
            hop(c, 0, -1).wait_recv()
            hop(c, -1, -1).start()
            across(c, 1).start()
            across(c, -1).start()

        @pl.when(inside(t + 1))
        def _():
            c = t + 1
            hop(c, 1, 1).wait_recv()
            across(c, 2).start()
            hop(c, -1, -1).wait_recv()
            across(c, -2).start()

        @pl.when(inside(t - 5))
        def _():
            c = t - 5
            hop(c, 2, 1).start()
            hop(c, -2, -1).start()

        @pl.when(inside(t - 6))
        def _():
            c = t - 6
            hop(c, 2, 1).wait_recv()
            hop(c, -2, -1).wait_recv()

            @pl.when(lax.rem(c, 2) == 0)
            def _():
                hop(c, 3, 1).start()

            @pl.when(lax.rem(c, 2) == 1)
            def _():
                hop(c, -3, -1).start()

            across(c, 3).start()
            across(c, -3).start()

        @pl.when(inside(t - 7))
        def _():
            c = t - 7
            hop(c, 3, 1).wait_recv()
            across(c, 4).start()

        @pl.when(t < 0)
        def _():
            @pl.loop(0, 43)
            def _(i):
                load_rows(jnp.minimum((t + 3) * 43 + i, COLS - 1))

        @pl.when(inside(t))
        def _():
            own_copy(t).wait()
            for dist in (0, 1, -1, 2):
                across(t, dist).wait_recv()
            compute(t, 0)

        @pl.when(t == STEPS)
        def _():
            send_result(0)

        @pl.when(t >= STEPS)
        def _():
            for dist in (-2, 3, -3, 4):
                across(t - STEPS, dist).wait_recv()
            compute(t - STEPS, 1)

    send_result(1)

    @pl.loop(0, STEPS)
    def _(c):
        for dist, step in ((0, 1), (0, -1), (1, 1), (-1, -1), (2, 1), (-2, -1), (3, 1)):
            hop(c, dist, step).wait_send()
        for dist in DIST.values():
            across(c, dist).wait_send()

    @pl.when(moved)
    def _():
        for tile in range(2):
            for piece in result_pieces(tile):
                result_remote(*piece).wait()

    @pl.when(jnp.logical_not(moved))
    def _():
        for tile in range(2):
            for piece in result_pieces(tile):
                result_local(*piece).wait()


def correlate_pairs(own, part, table):
    return pl.pallas_call(
        pair_kernel,
        out_shape=jax.ShapeDtypeStruct((CH, 16 * CH, LAGS), jnp.bfloat16),
        in_specs=[
            pl.BlockSpec(memory_space=pltpu.VMEM),
            pl.BlockSpec(memory_space=pl.ANY),
            pl.BlockSpec(memory_space=pltpu.VMEM),
        ],
        out_specs=pl.BlockSpec(memory_space=pl.ANY),
        scratch_shapes=[
            pltpu.VMEM((COLS, CH, COLS), jnp.float32),
            pltpu.VMEM((COLS, CH, COLS), jnp.float32),
            pltpu.VMEM((COLS, 16 * CH, COLS), jnp.bfloat16),
            pltpu.VMEM((CH * 16, COLS), jnp.bfloat16),
            pltpu.VMEM((CH, TILE, TILE), jnp.bfloat16),
            pltpu.VMEM((CH, LAGS, TILE), jnp.float32),
            pltpu.VMEM((2, CH, TILE, LAGS), jnp.bfloat16),
            pltpu.SemaphoreType.DMA((STEPS,)),
            pltpu.SemaphoreType.DMA((STEPS, 2, 8)),
            pltpu.SemaphoreType.DMA((STEPS, 15)),
            pltpu.SemaphoreType.DMA((16,)),
            pltpu.SemaphoreType.DMA((16,)),
        ],
        compiler_params=pltpu.CompilerParams(
            collective_id=0, has_side_effects=True, vmem_limit_bytes=60 << 20
        ),
        name="pairs",
    )(own, part, table)


def on_device(spectra, partner):
    whitened = whiten(spectra)
    rows = whitened.reshape(CH, WINDOWS, 2, INNER, COLS)
    rows = jnp.transpose(rows, (4, 0, 2, 3, 1)).reshape(COLS, CH, COLS)
    swap = [(0, 0), (1, 2), (2, 1), (3, 3)]
    own = lax.ppermute(rows, ("core", "ylo"), swap)
    groups = ("x", "yh", "ylo")
    spread = lax.all_to_all(
        own.reshape(16, COLS // 16, CH, COLS), groups, split_axis=0, concat_axis=0, tiled=True
    )
    ordered = jnp.take(spread, partner, axis=0)
    part = lax.all_to_all(ordered, groups, split_axis=0, concat_axis=0, tiled=True)
    return correlate_pairs(own, part.reshape(COLS, CH, COLS), lag_rows())


def solution(mesh):
    split = Mesh(mesh.devices.reshape(4, 2, 2, 2, 8), AXES)
    return jax.shard_map(
        on_device,
        mesh=split,
        in_specs=(P(AXES, None, None), P()),
        out_specs=P(AXES, None, None),
        check_vma=False,
    )
```

time: 633 us -> 285 us (0.45)
  blocking collectives: 221 us -> 0 us
  Pallas kernels: 0 us -> 215 us
  other arithmetic: 130 us -> 5.88 us
  matrix products: 102 us -> 0.74 us
  local copies, waits for them, and re-layouts: 74.2 us -> 8.38 us
  waiting for transfers between devices: 88.2 us -> 39.1 us
    all_to_all x3 -> x0, blocking collectives: 221 us -> none  [the longest x1 100 us: on_device(): lax.all_to_all(back_send, 'member', split_axis=0, concat_axis=0, tiled=True)]
    pallas_call x0 -> x1, Pallas kernels: none -> 215 us  [correlate_pairs(): pl.pallas_call(pair_kernel, out_shape=jax.ShapeDtypeStruct((CH, 16 * CH,...]
    concatenate x18 -> x0, other arithmetic: 121 us -> none  [the longest x8 117 us: correlate(): jnp.concatenate([cross_real, cross_imag], axis=2).astype(jnp.bfloat16)]
    dot_general x24 -> x0, matrix products: 102 us -> none  [the longest x8 47.3 us: correlate(): jnp.einsum('awf,bwf->abf', left_imag, right_part, preferred_element_type=...]
    all_to_all x2, waiting for transfers between devices: 88.2 us -> 26.5 us  [the longest x1 15.6 us: on_device(): lax.all_to_all(own.reshape(16, COLS // 16, CH, COLS), groups, split_axis=...]
    concatenate x8 -> x0, local copies, waits for them, and re-layouts: 38 us -> none  [correlate(): jnp.concatenate([other_rows[:, :, :freq_count], other_rows[:, :, freq_cou...]
    while x34 -> x0, local copies, waits for them, and re-layouts: 14.7 us -> none  [the longest x2 14.6 us: correlate_blocks(): lax.map(lambda portion: correlate(own_rows, portion, lag_table), stacked)]
    ppermute x0 -> x1, waiting for transfers between devices: none -> 12.6 us  [on_device(): own = lax.ppermute(rows, ('core', 'ylo'), swap)]
  transfers between devices with their start and end apart: 2 -> 3, of which waited for: 2 -> 3; matrix products, arithmetic and copies ran while one was open for 4% -> 1% of each run, Pallas kernels for 0% -> 0%
where the time goes in v1:
time: 285 us; the launch traced here: 284 us
  Pallas kernels  215 us (75%)
  waiting for transfers between devices  39.1 us (14%)
  starting transfers between devices  15.5 us (5%)
  local copies, waits for them, and re-layouts  8.38 us (3%)
  other arithmetic  5.88 us (2%)
    pallas_call x1, Pallas kernels, correlate_pairs(): pl.pallas_call(pair_kernel, out_shape=jax.ShapeDtypeStruct((CH, 16 * CH,...  215 us
    all_to_all x1, waiting for transfers between devices, on_device(): lax.all_to_all(own.reshape(16, COLS // 16, CH, COLS), groups, split_axis=...  15.6 us
    ppermute x1, waiting for transfers between devices, on_device(): own = lax.ppermute(rows, ('core', 'ylo'), swap)  12.6 us
    all_to_all x1, waiting for transfers between devices, on_device(): lax.all_to_all(ordered, groups, split_axis=0, concat_axis=0, tiled=True)  10.9 us
    all_to_all x1, starting transfers between devices, on_device(): lax.all_to_all(own.reshape(16, COLS // 16, CH, COLS), groups, split_axis=...  6.63 us
  transfers between devices with their start and end apart: 3, of which 3 were waited for; matrix products, arithmetic and copies ran while one was open for 1% of the time, Pallas kernels for 0%

profile of v1, /device:TPU:1, one launch (start us, length us, event | category | flops | bytes accessed | tf_op | source)
XLA Modules:
  0.0 284.4 jit_solution(3969748312832063654)
XLA Ops:
  0.0 0.0 copy-start
  0.0 1.7 add_reduce_fusion
  1.7 0.7 fusion.4
  2.5 0.0 copy-start.2
  2.5 0.0 copy-done
  2.5 0.3 fusion.5
  2.8 1.0 copy.4
  3.8 4.6 %collective-permute-start = (bf16[128,32,128]{2,1,0:T(8,128)(2,1)S(1)}, bf16[128,32,128]{2,1,0:T(8,128)(2,1)}, u32[]{:S(2)}, u32[]{:S(2)}) collective-permute-start(bf16[128,32,128]{2,1,0:T(8,128)(2,1)S(1)} %copy.4), channel_id=1, source_target_pairs={{0,0},{8,16},{16,8},{24,24},{1,1},{9,17},{17,9},{25,25},{2,2},{10,... | collective-permute-start | bytes 3145736 | tf_op jit(solution)/shard_map/ppermute | solution.py:349
  8.4 12.6 %collective-permute-done.own_ref = bf16[128,32,128]{2,1,0:T(8,128)(2,1)} collective-permute-done((bf16[128,32,128]{2,1,0:T(8,128)(2,1)S(1)}, bf16[128,32,128]{2,1,0:T(8,128)(2,1)}, u32[]{:S(2)}, u32[]{:S(2)}) %collective-permute-start) | collective-permute-done | bytes 1048608 | tf_op jit(solution)/shard_map/ppermute | solution.py:349
  21.0 6.6 %all-to-all-start = ((bf16[16,8,32,128]{3,2,1,0:T(8,128)(2,1)}), bf16[16,8,32,128]{3,2,1,0:T(8,128)(2,1)S(1)}, u32[]{:S(2)}, u32[]{:S(2)}) async-start(bf16[16,8,32,128]{3,2,1,0:T(8,128)(2,1)} %bitcast.3), calls=%async_computation | async-start | bytes 2097152 | tf_op jit(solution)/shard_map/all_to_all | solution.py:351
  27.6 0.0 copy-done.2
  27.7 15.6 %all-to-all-done = bf16[16,8,32,128]{3,2,1,0:T(8,128)(2,1)S(1)} async-done(((bf16[16,8,32,128]{3,2,1,0:T(8,128)(2,1)}), bf16[16,8,32,128]{3,2,1,0:T(8,128)(2,1)S(1)}, u32[]{:S(2)}, u32[]{:S(2)}) %all-to-all-start) | async-done | bytes 1048608 | tf_op jit(solution)/shard_map/all_to_all | solution.py:351
  43.3 0.7 gather_fusion
  44.0 1.1 broadcast_select_fusion
  45.2 4.3 %all-to-all-start.1 = ((bf16[16,8,32,128]{3,2,1,0:T(8,128)(2,1)}), bf16[16,8,32,128]{3,2,1,0:T(8,128)(2,1)S(1)}, u32[]{:S(2)}, u32[]{:S(2)}) async-start(bf16[16,8,32,128]{3,2,1,0:T(8,128)(2,1)} %broadcast_select_fusion), calls=%async_computation.1 | async-start | bytes 2097152 | tf_op jit(solution)/shard_map/all_to_all | solution.py:355
  49.5 0.1 broadcast_add_fusion
  49.6 2.5 multiply_convert_fusion.2
  52.1 0.1 pad_maximum_fusion
  52.2 1.0 copy.5.lag_ref
  53.2 10.9 %all-to-all-done.1 = bf16[16,8,32,128]{3,2,1,0:T(8,128)(2,1)S(1)} async-done(((bf16[16,8,32,128]{3,2,1,0:T(8,128)(2,1)}), bf16[16,8,32,128]{3,2,1,0:T(8,128)(2,1)S(1)}, u32[]{:S(2)}, u32[]{:S(2)}) %all-to-all-start.1) | async-done | bytes 1048608 | tf_op jit(solution)/shard_map/all_to_all | solution.py:355
  64.1 0.0 copy-start.1
  64.1 1.0 copy-done.1
  65.1 214.7 %pairs.1 = bf16[32,512,128]{2,1,0:T(8,128)(2,1)} custom-call(bf16[128,32,128]{2,1,0:T(8,128)(2,1)} %collective-permute-done.own_ref, bf16[128,32,128]{2,1,0:T(8,128)(2,1)} %bitcast.10, bf16[8,128,256]{2,1,0:T(8,128)(2,1)} %copy.5.lag_ref), custom_call_target="tpu_custom_call" | custom-call | tf_op jit(solution)/shard_map/pairs/pallas_call | solution.py:314
  279.8 4.7 %copy.7 = bf16[32,512,128]{2,1,0:T(8,128)(2,1)} copy(bf16[32,512,128]{2,1,0:T(8,128)(2,1)} %pairs.1) | data formatting | bytes 8388608
  (8 shorter events, 0.1 us)
Async XLA Ops:
  0.0 2.5 copy-start
  2.5 25.2 %copy-start.2 = (s32[16]{0:T(128)S(1)}, s32[16]{0:T(128)}, u32[]{:S(2)}) copy-start(s32[16]{0:T(128)} %param.3) | copy-start | bytes 196
  3.8 17.2 %collective-permute-start = (bf16[128,32,128]{2,1,0:T(8,128)(2,1)S(1)}, bf16[128,32,128]{2,1,0:T(8,128)(2,1)}, u32[]{:S(2)}, u32[]{:S(2)}) collective-permute-start(bf16[128,32,128]{2,1,0:T(8,128)(2,1)S(1)} %copy.4), channel_id=1, source_target_pairs={{0,0},{8,16},{16,8},{24,24},{1,1},{9,17},{17,9},{25,25},{2,2},{10,... | collective-permute-start | bytes 3145736 | tf_op jit(solution)/shard_map/ppermute | solution.py:349
  21.0 22.3 %all-to-all-start = ((bf16[16,8,32,128]{3,2,1,0:T(8,128)(2,1)}), bf16[16,8,32,128]{3,2,1,0:T(8,128)(2,1)S(1)}, u32[]{:S(2)}, u32[]{:S(2)}) async-start(bf16[16,8,32,128]{3,2,1,0:T(8,128)(2,1)} %bitcast.3), calls=%async_computation | async-start | bytes 2097152 | tf_op jit(solution)/shard_map/all_to_all | solution.py:351
  45.2 19.0 %all-to-all-start.1 = ((bf16[16,8,32,128]{3,2,1,0:T(8,128)(2,1)}), bf16[16,8,32,128]{3,2,1,0:T(8,128)(2,1)S(1)}, u32[]{:S(2)}, u32[]{:S(2)}) async-start(bf16[16,8,32,128]{3,2,1,0:T(8,128)(2,1)} %broadcast_select_fusion), calls=%async_computation.1 | async-start | bytes 2097152 | tf_op jit(solution)/shard_map/all_to_all | solution.py:355
  64.1 1.0 copy-start.1

commit v2 on v1

--- a/solution.py
+++ b/solution.py
@@ -19,6 +19,8 @@
 CHUNK = 16
 STEPS = COLS // CHUNK
 TILE = 256
+GROUP_COLS = 4
+GROUP_CH = 8
 AXES = ("x", "yh", "core", "ylo", "z")
 MESH = pl.DeviceIdType.MESH
 
@@ -160,7 +162,7 @@
         x_rows[column] = value
         xs_rows[column] = pltpu.roll(value, 64, 1) * sign
 
-    def cross_column(c, i, tile):
+    def cross_column(c, i, lane_slot, tile):
         column = c * CHUNK + i
         for a in range(CH):
             re_row = jnp.broadcast_to(x_rows[column, pl.ds(a, 1), :], (INNER, COLS))
@@ -168,40 +170,36 @@
             block = jnp.concatenate(
                 [jnp.where(mask, re_row, 0.0), jnp.where(mask, im_row, 0.0)], axis=0
             )
-            left[pl.ds(a * 16, 16), :] = block.astype(jnp.bfloat16)
+            left[lane_slot, pl.ds(a * 16, 16), :] = block.astype(jnp.bfloat16)
         right = gathered[column, pl.ds(pl.multiple_of(tile * TILE, TILE), TILE), :]
         product = lax.dot_general(
-            left[...], right, (((1,), (1,)), ((), ())), preferred_element_type=jnp.float32
+            left[lane_slot], right, (((1,), (1,)), ((), ())), preferred_element_type=jnp.float32
         )
         cross[:, pl.ds(pl.multiple_of(i * 16, 16), 16), :] = product.astype(
             jnp.bfloat16
         ).reshape(CH, 16, TILE)
 
-    def lag_channel(c, a, first):
+    def lag_channel(c, a):
         product = jnp.dot(lag_ref[c], cross[a], preferred_element_type=jnp.float32)
-
-        @pl.when(first)
-        def _():
-            total[a] = product
-
-        @pl.when(jnp.logical_not(first))
-        def _():
-            total[a] = total[a] + product
+        total[a] = jnp.where(c > 0, total[a], 0.0) + product
 
     def compute(c, tile):
-        @pl.loop(0, CHUNK)
+        @pl.loop(0, CHUNK // GROUP_COLS)
         def _(i):
-            cross_column(c, i, tile)
-
-        @pl.loop(0, CH)
-        def _(a):
-            lag_channel(c, a, c == 0)
+            for u in range(GROUP_COLS):
+                cross_column(c, i * GROUP_COLS + u, u, tile)
+
+        @pl.loop(0, CH // GROUP_CH)
+        def _(i):
+            for u in range(GROUP_CH):
+                lag_channel(c, i * GROUP_CH + u)
 
         @pl.when(c == STEPS - 1)
         def _():
-            @pl.loop(0, CH)
-            def _(a):
-                result[tile, a] = total[a].T.astype(jnp.bfloat16)
+            @pl.loop(0, CH // 4)
+            def _(i):
+                for u in range(4):
+                    result[tile, i * 4 + u] = total[i * 4 + u].T.astype(jnp.bfloat16)
 
     def inside(c):
         return jnp.logical_and(c >= 0, c < STEPS)
@@ -324,7 +322,7 @@
             pltpu.VMEM((COLS, CH, COLS), jnp.float32),
             pltpu.VMEM((COLS, CH, COLS), jnp.float32),
             pltpu.VMEM((COLS, 16 * CH, COLS), jnp.bfloat16),
-            pltpu.VMEM((CH * 16, COLS), jnp.bfloat16),
+            pltpu.VMEM((GROUP_COLS, CH * 16, COLS), jnp.bfloat16),
             pltpu.VMEM((CH, TILE, TILE), jnp.bfloat16),
             pltpu.VMEM((CH, LAGS, TILE), jnp.float32),
             pltpu.VMEM((2, CH, TILE, LAGS), jnp.bfloat16),

time: 285 us -> 205 us (0.72)
  Pallas kernels: 215 us -> 135 us
    pallas_call x1, Pallas kernels: 215 us -> 135 us  [correlate_pairs(): pl.pallas_call(pair_kernel, out_shape=jax.ShapeDtypeStruct((CH, 16 * CH,...]
  transfers between devices with their start and end apart: 3 -> 3, of which waited for: 3 -> 3; matrix products, arithmetic and copies ran while one was open for 1% -> 2% of each run, Pallas kernels for 0% -> 0%
where the time goes in v2:
time: 205 us; the launch traced here: 204 us
  Pallas kernels  135 us (66%)
  waiting for transfers between devices  39.1 us (19%)
  starting transfers between devices  15.5 us (8%)
  local copies, waits for them, and re-layouts  8.38 us (4%)
  other arithmetic  5.88 us (3%)
    pallas_call x1, Pallas kernels, correlate_pairs(): pl.pallas_call(pair_kernel, out_shape=jax.ShapeDtypeStruct((CH, 16 * CH,...  135 us
    all_to_all x1, waiting for transfers between devices, on_device(): lax.all_to_all(own.reshape(16, COLS // 16, CH, COLS), groups, split_axis=...  15.6 us
    ppermute x1, waiting for transfers between devices, on_device(): own = lax.ppermute(rows, ('core', 'ylo'), swap)  12.6 us
    all_to_all x1, waiting for transfers between devices, on_device(): lax.all_to_all(ordered, groups, split_axis=0, concat_axis=0, tiled=True)  10.9 us
    all_to_all x1, starting transfers between devices, on_device(): lax.all_to_all(own.reshape(16, COLS // 16, CH, COLS), groups, split_axis=...  6.63 us
    unnamed x7, local copies, waits for them, and re-layouts  5.63 us
    ppermute x1, starting transfers between devices, on_device(): own = lax.ppermute(rows, ('core', 'ylo'), swap)  4.59 us
    all_to_all x1, starting transfers between devices, on_device(): lax.all_to_all(ordered, groups, split_axis=0, concat_axis=0, tiled=True)  4.27 us
  transfers between devices with their start and end apart: 3, of which 3 were waited for; matrix products, arithmetic and copies ran while one was open for 2% of the time, Pallas kernels for 0%

profile of v2, /device:TPU:1, one launch (start us, length us, event | category | flops | bytes accessed | tf_op | source)
XLA Modules:
  0.0 204.4 jit_solution(14135284707349445760)
XLA Ops:
  0.0 0.0 copy-start
  0.0 1.7 add_reduce_fusion
  1.7 0.7 fusion.4
  2.5 0.0 copy-start.2
  2.5 0.0 copy-done
  2.5 0.3 fusion.5
  2.8 1.0 copy.4
  3.8 4.6 %collective-permute-start = (bf16[128,32,128]{2,1,0:T(8,128)(2,1)S(1)}, bf16[128,32,128]{2,1,0:T(8,128)(2,1)}, u32[]{:S(2)}, u32[]{:S(2)}) collective-permute-start(bf16[128,32,128]{2,1,0:T(8,128)(2,1)S(1)} %copy.4), channel_id=1, source_target_pairs={{0,0},{8,16},{16,8},{24,24},{1,1},{9,17},{17,9},{25,25},{2,2},{10,... | collective-permute-start | bytes 3145736 | tf_op jit(solution)/shard_map/ppermute | solution.py:347
  8.4 12.6 %collective-permute-done.own_ref = bf16[128,32,128]{2,1,0:T(8,128)(2,1)} collective-permute-done((bf16[128,32,128]{2,1,0:T(8,128)(2,1)S(1)}, bf16[128,32,128]{2,1,0:T(8,128)(2,1)}, u32[]{:S(2)}, u32[]{:S(2)}) %collective-permute-start) | collective-permute-done | bytes 1048608 | tf_op jit(solution)/shard_map/ppermute | solution.py:347
  21.0 6.6 %all-to-all-start = ((bf16[16,8,32,128]{3,2,1,0:T(8,128)(2,1)}), bf16[16,8,32,128]{3,2,1,0:T(8,128)(2,1)S(1)}, u32[]{:S(2)}, u32[]{:S(2)}) async-start(bf16[16,8,32,128]{3,2,1,0:T(8,128)(2,1)} %bitcast.3), calls=%async_computation | async-start | bytes 2097152 | tf_op jit(solution)/shard_map/all_to_all | solution.py:349
  27.6 0.0 copy-done.2
  27.7 15.6 %all-to-all-done = bf16[16,8,32,128]{3,2,1,0:T(8,128)(2,1)S(1)} async-done(((bf16[16,8,32,128]{3,2,1,0:T(8,128)(2,1)}), bf16[16,8,32,128]{3,2,1,0:T(8,128)(2,1)S(1)}, u32[]{:S(2)}, u32[]{:S(2)}) %all-to-all-start) | async-done | bytes 1048608 | tf_op jit(solution)/shard_map/all_to_all | solution.py:349
  43.3 0.7 gather_fusion
  44.0 1.1 broadcast_select_fusion
  45.2 4.3 %all-to-all-start.1 = ((bf16[16,8,32,128]{3,2,1,0:T(8,128)(2,1)}), bf16[16,8,32,128]{3,2,1,0:T(8,128)(2,1)S(1)}, u32[]{:S(2)}, u32[]{:S(2)}) async-start(bf16[16,8,32,128]{3,2,1,0:T(8,128)(2,1)} %broadcast_select_fusion), calls=%async_computation.1 | async-start | bytes 2097152 | tf_op jit(solution)/shard_map/all_to_all | solution.py:353
  49.5 0.1 broadcast_add_fusion
  49.6 2.5 %multiply_convert_fusion.2 = (bf16[8,128,16,1,8]{1,4,3,2,0:T(8,128)(2,1)S(1)}, bf16[8,128,16,1,8]{1,4,3,2,0:T(8,128)(2,1)S(1)}) fusion(s32[128]{0:T(128)S(1)} %iota_add_fusion.2, s32[8,16,8]{2,1,0:T(8,128)S(1)} %broadcast_add_fusion), kind=kLoop, calls=%fused_computation.21 | loop fusion | flops 2490368 | bytes 528896 | tf_op jit(solution)/shard_map/convert
  52.1 0.1 pad_maximum_fusion
  52.2 1.0 copy.5.lag_ref
  53.2 10.9 %all-to-all-done.1 = bf16[16,8,32,128]{3,2,1,0:T(8,128)(2,1)S(1)} async-done(((bf16[16,8,32,128]{3,2,1,0:T(8,128)(2,1)}), bf16[16,8,32,128]{3,2,1,0:T(8,128)(2,1)S(1)}, u32[]{:S(2)}, u32[]{:S(2)}) %all-to-all-start.1) | async-done | bytes 1048608 | tf_op jit(solution)/shard_map/all_to_all | solution.py:353
  64.1 0.0 copy-start.1
  64.1 1.0 copy-done.1
  65.1 134.6 %pairs.1 = bf16[32,512,128]{2,1,0:T(8,128)(2,1)} custom-call(bf16[128,32,128]{2,1,0:T(8,128)(2,1)} %collective-permute-done.own_ref, bf16[128,32,128]{2,1,0:T(8,128)(2,1)} %bitcast.10, bf16[8,128,256]{2,1,0:T(8,128)(2,1)} %copy.5.lag_ref), custom_call_target="tpu_custom_call" | custom-call | tf_op jit(solution)/shard_map/pairs/pallas_call | solution.py:312
  199.7 4.7 %copy.7 = bf16[32,512,128]{2,1,0:T(8,128)(2,1)} copy(bf16[32,512,128]{2,1,0:T(8,128)(2,1)} %pairs.1) | data formatting | bytes 8388608
  (8 shorter events, 0.1 us)
Async XLA Ops:
  0.0 2.5 %copy-start = (bf16[32,8,2048]{2,1,0:T(8,128)(2,1)S(1)}, bf16[32,8,2048]{2,1,0:T(8,128)(2,1)}, u32[]{:S(2)}) copy-start(bf16[32,8,2048]{2,1,0:T(8,128)(2,1)} %param.2) | copy-start | bytes 3145732
  2.5 25.2 %copy-start.2 = (s32[16]{0:T(128)S(1)}, s32[16]{0:T(128)}, u32[]{:S(2)}) copy-start(s32[16]{0:T(128)} %param.3) | copy-start | bytes 196
  3.8 17.2 %collective-permute-start = (bf16[128,32,128]{2,1,0:T(8,128)(2,1)S(1)}, bf16[128,32,128]{2,1,0:T(8,128)(2,1)}, u32[]{:S(2)}, u32[]{:S(2)}) collective-permute-start(bf16[128,32,128]{2,1,0:T(8,128)(2,1)S(1)} %copy.4), channel_id=1, source_target_pairs={{0,0},{8,16},{16,8},{24,24},{1,1},{9,17},{17,9},{25,25},{2,2},{10,... | collective-permute-start | bytes 3145736 | tf_op jit(solution)/shard_map/ppermute | solution.py:347
  21.0 22.3 %all-to-all-start = ((bf16[16,8,32,128]{3,2,1,0:T(8,128)(2,1)}), bf16[16,8,32,128]{3,2,1,0:T(8,128)(2,1)S(1)}, u32[]{:S(2)}, u32[]{:S(2)}) async-start(bf16[16,8,32,128]{3,2,1,0:T(8,128)(2,1)} %bitcast.3), calls=%async_computation | async-start | bytes 2097152 | tf_op jit(solution)/shard_map/all_to_all | solution.py:349
  45.2 19.0 %all-to-all-start.1 = ((bf16[16,8,32,128]{3,2,1,0:T(8,128)(2,1)}), bf16[16,8,32,128]{3,2,1,0:T(8,128)(2,1)S(1)}, u32[]{:S(2)}, u32[]{:S(2)}) async-start(bf16[16,8,32,128]{3,2,1,0:T(8,128)(2,1)} %broadcast_select_fusion), calls=%async_computation.1 | async-start | bytes 2097152 | tf_op jit(solution)/shard_map/all_to_all | solution.py:353
  64.1 1.0 copy-start.1

commit v3 on v2

--- a/solution.py
+++ b/solution.py
@@ -3,6 +3,7 @@
 
 import jax
 import jax.numpy as jnp
+import numpy as np
 from jax import lax
 from jax.experimental import pallas as pl
 from jax.experimental.pallas import tpu as pltpu
@@ -51,58 +52,169 @@
 
 
 def lag_rows():
-    lag_values = jnp.arange(LAGS, dtype=jnp.int32) - LAGS // 2
-    columns = jnp.arange(COLS, dtype=jnp.int32).reshape(STEPS, CHUNK)
-    freq = columns[:, :, None] + COLS * jnp.arange(INNER, dtype=jnp.int32)[None, None, :]
-    residue = jnp.mod(freq[:, None, :, :] * lag_values[None, :, None, None], 2 * FREQS)
-    angles = jnp.pi * residue.astype(jnp.float32) / FREQS
+    lag_values = np.arange(LAGS) - LAGS // 2
+    columns = np.arange(COLS).reshape(STEPS, CHUNK)
+    freq = columns[:, :, None] + COLS * np.arange(INNER)[None, None, :]
+    residue = np.mod(freq[:, None, :, :] * lag_values[None, :, None, None], 2 * FREQS)
+    angles = np.pi * residue / FREQS
     norm_factor = 1.0 / math.sqrt(WINDOWS * FREQS)
-    table = jnp.stack([jnp.cos(angles) * norm_factor, -jnp.sin(angles) * norm_factor], axis=3)
+    table = np.stack([np.cos(angles) * norm_factor, -np.sin(angles) * norm_factor], axis=3)
     return table.reshape(STEPS, LAGS, CHUNK * 2 * INNER).astype(jnp.bfloat16)
 
 
 def pair_kernel(
-    own_ref, part_ref, lag_ref, out_ref,
-    x_rows, xs_rows, gathered, left, cross, total, result,
-    own_sem, recv_sem, send_sem, out_send, out_recv,
+    partner_ref, rows_ref, lag_ref, out_ref,
+    spread, ordered, own, x_rows, xs_rows, gathered, left, cross, total, result,
+    local_sem, spread_send, spread_recv, own_send, own_recv, part_send, part_recv,
+    recv_sem, send_sem, out_send, out_recv,
 ):
+    x = lax.axis_index("x")
+    yh = lax.axis_index("yh")
     core = lax.axis_index("core")
     ylo = lax.axis_index("ylo")
     z = lax.axis_index("z")
     up = lax.rem(z + 1, 8)
     down = lax.rem(z + 7, 8)
     moved = core != ylo
+    chip = x * 2 + yh
+    group = chip * 2 + core
+    mirror = {"core": ylo, "ylo": core}
 
     barrier = pltpu.get_barrier_semaphore()
+    plane = group * 2 + ylo
+    for i in range(1, 32):
+        other = lax.rem(plane + i, 32)
+        where = {
+            "x": other // 8, "yh": lax.rem(other // 4, 2),
+            "core": lax.rem(other // 2, 2), "ylo": lax.rem(other, 2),
+        }
+        pl.semaphore_signal(barrier, inc=1, device_id=where, device_id_type=MESH)
     pl.semaphore_signal(barrier, inc=1, device_id={"z": up}, device_id_type=MESH)
     pl.semaphore_signal(barrier, inc=1, device_id={"z": down}, device_id_type=MESH)
-    pl.semaphore_signal(barrier, inc=1, device_id={"core": 1 - core}, device_id_type=MESH)
+    pl.semaphore_wait(barrier, 33)
+
+    def share(t):
+        to = lax.rem(group + t, 16)
+        return pltpu.make_async_remote_copy(
+            src_ref=rows_ref.at[pl.ds(pl.multiple_of(to * 8, 8), 8)],
+            dst_ref=spread.at[group],
+            send_sem=spread_send.at[t],
+            recv_sem=spread_recv.at[group],
+            device_id={"x": to // 4, "yh": lax.rem(to // 2, 2), "core": lax.rem(to, 2)},
+            device_id_type=MESH,
+        )
+
+    def share_from(t):
+        source = lax.rem(group + t, 16)
+        return pltpu.make_async_remote_copy(
+            src_ref=rows_ref.at[pl.ds(0, 8)],
+            dst_ref=spread.at[source],
+            send_sem=spread_send.at[t],
+            recv_sem=spread_recv.at[source],
+            device_id={"core": 1 - core},
+            device_id_type=MESH,
+        )
+
+    own_share = pltpu.make_async_copy(
+        rows_ref.at[pl.ds(pl.multiple_of(group * 8, 8), 8)], spread.at[group], local_sem.at[0]
+    )
+    own_swap = pltpu.make_async_remote_copy(
+        src_ref=rows_ref, dst_ref=own, send_sem=own_send, recv_sem=own_recv,
+        device_id=mirror, device_id_type=MESH,
+    )
+    own_stay = pltpu.make_async_copy(rows_ref, own, local_sem.at[1])
+
+    own_share.start()
+    for t in range(1, 16):
+        share(t).start()
 
     @pl.when(moved)
     def _():
-        pl.semaphore_signal(
-            barrier, inc=1, device_id={"core": ylo, "ylo": core}, device_id_type=MESH
-        )
-        pl.semaphore_wait(barrier, 4)
+        own_swap.start()
 
     @pl.when(jnp.logical_not(moved))
     def _():
-        pl.semaphore_wait(barrier, 3)
+        own_stay.start()
+
+    own_share.wait()
+    for t in range(1, 16):
+        share_from(t).wait_recv()
+
+    for g in range(16):
+        ordered[g] = spread[partner_ref[g]]
 
     def columns(c):
-        return pl.ds(pl.multiple_of(c * CHUNK, CHUNK), CHUNK)
+        step = lax.rem(c + chip, STEPS)
+        return pl.ds(pl.multiple_of(step * CHUNK, CHUNK), CHUNK)
 
     def place(c, dist, member):
         start = SLOT[dist] * 64 + member * 32
         return gathered.at[columns(c), pl.ds(pl.multiple_of(start, 32), 32), :]
 
-    def source(c, dist):
-        return part_ref.at[columns(c)] if dist == 0 else place(c, dist, core)
+    def share_place(source, member):
+        cols = pl.ds(pl.multiple_of(source * 8, 8), 8)
+        return gathered.at[cols, pl.ds(pl.multiple_of(member * 32, 32), 32), :]
+
+    def give(t, member):
+        to = lax.rem(chip + 8 - t, 8)
+        return pltpu.make_async_remote_copy(
+            src_ref=ordered.at[to * 2 + member],
+            dst_ref=share_place(group, ylo),
+            send_sem=part_send.at[t * 2 + member],
+            recv_sem=part_recv.at[group],
+            device_id={"x": to // 2, "yh": lax.rem(to, 2), "core": ylo, "ylo": member},
+            device_id_type=MESH,
+        )
+
+    def keep(member):
+        return pltpu.make_async_copy(
+            ordered.at[chip * 2 + member], share_place(group, ylo), local_sem.at[2]
+        )
+
+    def take(c, source_core):
+        source = lax.rem(chip + c, 8) * 2 + source_core
+        return pltpu.make_async_remote_copy(
+            src_ref=ordered.at[0],
+            dst_ref=share_place(source, core),
+            send_sem=part_send.at[0],
+            recv_sem=part_recv.at[source],
+            device_id={"core": 1 - core},
+            device_id_type=MESH,
+        )
+
+    for member in range(2):
+        stays = jnp.logical_and(jnp.logical_not(moved), ylo == member)
+
+        @pl.when(stays)
+        def _():
+            keep(member).start()
+
+        @pl.when(jnp.logical_not(stays))
+        def _():
+            give(0, member).start()
+
+    for t in range(1, 8):
+        for member in range(2):
+            give(t, member).start()
+
+    def wait_part(c):
+        for source_core in range(2):
+            stays = jnp.logical_and(
+                c == 0, jnp.logical_and(jnp.logical_not(moved), core == source_core)
+            )
+
+            @pl.when(stays)
+            def _():
+                keep(source_core).wait()
+
+            @pl.when(jnp.logical_not(stays))
+            def _():
+                take(c, source_core).wait_recv()
 
     def hop(c, dist, step):
         landed = 4 if dist + step == -4 else dist + step
         return pltpu.make_async_remote_copy(
-            src_ref=source(c, dist),
+            src_ref=place(c, dist, core),
             dst_ref=place(c, landed, core),
             send_sem=send_sem.at[c, SLOT[landed] - 1],
             recv_sem=recv_sem.at[c, 0, SLOT[landed]],
@@ -112,7 +224,7 @@
 
     def across(c, dist):
         return pltpu.make_async_remote_copy(
-            src_ref=source(c, dist),
+            src_ref=place(c, dist, core),
             dst_ref=place(c, dist, core),
             send_sem=send_sem.at[c, 7 + SLOT[dist]],
             recv_sem=recv_sem.at[c, 1, SLOT[dist]],
@@ -120,8 +232,15 @@
             device_id_type=MESH,
         )
 
-    def own_copy(c):
-        return pltpu.make_async_copy(part_ref.at[columns(c)], place(c, 0, core), own_sem.at[c])
+    def across_in(c, dist):
+        return pltpu.make_async_remote_copy(
+            src_ref=place(c, dist, core),
+            dst_ref=place(c, dist, 1 - core),
+            send_sem=send_sem.at[c, 7 + SLOT[dist]],
+            recv_sem=recv_sem.at[c, 1, SLOT[dist]],
+            device_id={"core": 1 - core},
+            device_id_type=MESH,
+        )
 
     def result_pieces(tile):
         for piece in range(4):
@@ -135,7 +254,7 @@
         return pltpu.make_async_remote_copy(
             src_ref=src, dst_ref=out_ref.at[:, target, :],
             send_sem=out_send.at[index], recv_sem=out_recv.at[index],
-            device_id={"core": ylo, "ylo": core}, device_id_type=MESH,
+            device_id=mirror, device_id_type=MESH,
         )
 
     def result_local(index, src, target):
@@ -158,12 +277,12 @@
     sign = jnp.where(lax.broadcasted_iota(jnp.int32, (CH, COLS), 1) < 64, 1.0, -1.0)
 
     def load_rows(column):
-        value = own_ref[column].astype(jnp.float32)
+        value = own[column].astype(jnp.float32)
         x_rows[column] = value
         xs_rows[column] = pltpu.roll(value, 64, 1) * sign
 
     def cross_column(c, i, lane_slot, tile):
-        column = c * CHUNK + i
+        column = lax.rem(c + chip, STEPS) * CHUNK + i
         for a in range(CH):
             re_row = jnp.broadcast_to(x_rows[column, pl.ds(a, 1), :], (INNER, COLS))
             im_row = jnp.broadcast_to(xs_rows[column, pl.ds(a, 1), :], (INNER, COLS))
@@ -180,7 +299,7 @@
         ).reshape(CH, 16, TILE)
 
     def lag_channel(c, a):
-        product = jnp.dot(lag_ref[c], cross[a], preferred_element_type=jnp.float32)
+        product = jnp.dot(lag_ref[lax.rem(c + chip, STEPS)], cross[a], preferred_element_type=jnp.float32)
         total[a] = jnp.where(c > 0, total[a], 0.0) + product
 
     def compute(c, tile):
@@ -204,21 +323,13 @@
     def inside(c):
         return jnp.logical_and(c >= 0, c < STEPS)
 
-    @pl.loop(0, 2 * STEPS + 3)
+    @pl.loop(0, 2 * STEPS + 5)
     def _(tick):
-        t = tick - 3
+        t = tick - 5
 
         @pl.when(inside(t + 3))
         def _():
             c = t + 3
-            own_copy(c).start()
-            hop(c, 0, 1).start()
-            hop(c, 0, -1).start()
-            across(c, 0).start()
-
-        @pl.when(inside(t + 2))
-        def _():
-            c = t + 2
             hop(c, 0, 1).wait_recv()
             hop(c, 1, 1).start()
             hop(c, 0, -1).wait_recv()
@@ -226,6 +337,14 @@
             across(c, 1).start()
             across(c, -1).start()
 
+        @pl.when(inside(t + 5))
+        def _():
+            c = t + 5
+            wait_part(c)
+            hop(c, 0, 1).start()
+            hop(c, 0, -1).start()
+            across(c, 0).start()
+
         @pl.when(inside(t + 1))
         def _():
             c = t + 1
@@ -234,15 +353,15 @@
             hop(c, -1, -1).wait_recv()
             across(c, -2).start()
 
-        @pl.when(inside(t - 5))
-        def _():
-            c = t - 5
+        @pl.when(inside(t - 3))
+        def _():
+            c = t - 3
             hop(c, 2, 1).start()
             hop(c, -2, -1).start()
 
-        @pl.when(inside(t - 6))
-        def _():
-            c = t - 6
+        @pl.when(inside(t - 5))
+        def _():
+            c = t - 5
             hop(c, 2, 1).wait_recv()
             hop(c, -2, -1).wait_recv()
 
@@ -263,7 +382,17 @@
             hop(c, 3, 1).wait_recv()
             across(c, 4).start()
 
-        @pl.when(t < 0)
+        @pl.when(t == -3)
+        def _():
+            @pl.when(moved)
+            def _():
+                own_swap.wait_recv()
+
+            @pl.when(jnp.logical_not(moved))
+            def _():
+                own_stay.wait()
+
+        @pl.when(jnp.logical_and(t >= -3, t < 0))
         def _():
             @pl.loop(0, 43)
             def _(i):
@@ -271,9 +400,8 @@
 
         @pl.when(inside(t))
         def _():
-            own_copy(t).wait()
             for dist in (0, 1, -1, 2):
-                across(t, dist).wait_recv()
+                across_in(t, dist).wait_recv()
             compute(t, 0)
 
         @pl.when(t == STEPS)
@@ -283,10 +411,26 @@
         @pl.when(t >= STEPS)
         def _():
             for dist in (-2, 3, -3, 4):
-                across(t - STEPS, dist).wait_recv()
+                across_in(t - STEPS, dist).wait_recv()
             compute(t - STEPS, 1)
 
     send_result(1)
+
+    for t in range(1, 16):
+        share(t).wait_send()
+
+    @pl.when(moved)
+    def _():
+        own_swap.wait_send()
+
+    for member in range(2):
+        @pl.when(jnp.logical_or(moved, ylo != member))
+        def _():
+            give(0, member).wait_send()
+
+    for t in range(1, 8):
+        for member in range(2):
+            give(t, member).wait_send()
 
     @pl.loop(0, STEPS)
     def _(c):
@@ -308,17 +452,20 @@
                 result_local(*piece).wait()
 
 
-def correlate_pairs(own, part, table):
+def correlate_pairs(partner, rows, table):
     return pl.pallas_call(
         pair_kernel,
         out_shape=jax.ShapeDtypeStruct((CH, 16 * CH, LAGS), jnp.bfloat16),
         in_specs=[
-            pl.BlockSpec(memory_space=pltpu.VMEM),
+            pl.BlockSpec(memory_space=pltpu.SMEM),
             pl.BlockSpec(memory_space=pl.ANY),
             pl.BlockSpec(memory_space=pltpu.VMEM),
         ],
         out_specs=pl.BlockSpec(memory_space=pl.ANY),
         scratch_shapes=[
+            pltpu.VMEM((16, 8, CH, COLS), jnp.bfloat16),
+            pltpu.VMEM((16, 8, CH, COLS), jnp.bfloat16),
+            pltpu.VMEM((COLS, CH, COLS), jnp.bfloat16),
             pltpu.VMEM((COLS, CH, COLS), jnp.float32),
             pltpu.VMEM((COLS, CH, COLS), jnp.float32),
             pltpu.VMEM((COLS, 16 * CH, COLS), jnp.bfloat16),
@@ -326,7 +473,13 @@
             pltpu.VMEM((CH, TILE, TILE), jnp.bfloat16),
             pltpu.VMEM((CH, LAGS, TILE), jnp.float32),
             pltpu.VMEM((2, CH, TILE, LAGS), jnp.bfloat16),
-            pltpu.SemaphoreType.DMA((STEPS,)),
+            pltpu.SemaphoreType.DMA((3,)),
+            pltpu.SemaphoreType.DMA((16,)),
+            pltpu.SemaphoreType.DMA((16,)),
+            pltpu.SemaphoreType.DMA,
+            pltpu.SemaphoreType.DMA,
+            pltpu.SemaphoreType.DMA((16,)),
+            pltpu.SemaphoreType.DMA((16,)),
             pltpu.SemaphoreType.DMA((STEPS, 2, 8)),
             pltpu.SemaphoreType.DMA((STEPS, 15)),
             pltpu.SemaphoreType.DMA((16,)),
@@ -336,22 +489,14 @@
             collective_id=0, has_side_effects=True, vmem_limit_bytes=60 << 20
         ),
         name="pairs",
-    )(own, part, table)
+    )(partner, rows, table)
 
 
 def on_device(spectra, partner):
     whitened = whiten(spectra)
     rows = whitened.reshape(CH, WINDOWS, 2, INNER, COLS)
     rows = jnp.transpose(rows, (4, 0, 2, 3, 1)).reshape(COLS, CH, COLS)
-    swap = [(0, 0), (1, 2), (2, 1), (3, 3)]
-    own = lax.ppermute(rows, ("core", "ylo"), swap)
-    groups = ("x", "yh", "ylo")
-    spread = lax.all_to_all(
-        own.reshape(16, COLS // 16, CH, COLS), groups, split_axis=0, concat_axis=0, tiled=True
-    )
-    ordered = jnp.take(spread, partner, axis=0)
-    part = lax.all_to_all(ordered, groups, split_axis=0, concat_axis=0, tiled=True)
-    return correlate_pairs(own, part.reshape(COLS, CH, COLS), lag_rows())
+    return correlate_pairs(partner, rows, jnp.asarray(lag_rows()))
 
 
 def solution(mesh):

time: 205 us -> 178 us (0.87)
  waiting for transfers between devices: 39.1 us -> 0 us
  Pallas kernels: 135 us -> 168 us
  starting transfers between devices: 15.5 us -> 0 us
  other arithmetic: 5.88 us -> 2.05 us
  local copies, waits for them, and re-layouts: 8.38 us -> 6.33 us
    pallas_call x1, Pallas kernels: 135 us -> 168 us  [correlate_pairs(): pl.pallas_call(pair_kernel, out_shape=jax.ShapeDtypeStruct((CH, 16 * CH,...]
    all_to_all x2 -> x0, waiting for transfers between devices: 26.5 us -> none  [the longest x1 15.6 us: on_device(): lax.all_to_all(own.reshape(16, COLS // 16, CH, COLS), groups, split_axis=...]
    ppermute x1 -> x0, waiting for transfers between devices: 12.6 us -> none  [on_device(): own = lax.ppermute(rows, ('core', 'ylo'), swap)]
    all_to_all x2 -> x0, starting transfers between devices: 10.9 us -> none  [the longest x1 6.63 us: on_device(): lax.all_to_all(own.reshape(16, COLS // 16, CH, COLS), groups, split_axis=...]
    ppermute x1 -> x0, starting transfers between devices: 4.59 us -> none  [on_device(): own = lax.ppermute(rows, ('core', 'ylo'), swap)]
    another operation x3 -> x0, other arithmetic: 2.59 us -> none
    unnamed x7 -> x3, local copies, waits for them, and re-layouts: 5.63 us -> 4.66 us
  transfers between devices with their start and end apart: 3 -> 0, of which waited for: 3 -> 0; matrix products, arithmetic and copies ran while one was open for 2% -> 0% of each run, Pallas kernels for 0% -> 0%
where the time goes in v3:
time: 178 us; the launch traced here: 177 us
  Pallas kernels  168 us (94%)
  local copies, waits for them, and re-layouts  6.33 us (4%)
  other arithmetic  2.05 us (1%)
    pallas_call x1, Pallas kernels, correlate_pairs(): pl.pallas_call(pair_kernel, out_shape=jax.ShapeDtypeStruct((CH, 16 * CH,...  168 us
    unnamed x3, local copies, waits for them, and re-layouts  4.66 us

profile of v3, /device:TPU:1, one launch (start us, length us, event | category | flops | bytes accessed | tf_op | source)
XLA Modules:
  0.0 177.4 jit_solution(9094578938139589868)
XLA Ops:
  0.0 0.0 copy-start
  0.0 1.7 add_reduce_fusion
  1.7 0.7 fusion.4
  2.5 0.0 copy-done
  2.5 0.3 fusion.5
  2.8 1.7 copy.5.rows_ref
  4.5 168.3 %pairs.1 = bf16[32,512,128]{2,1,0:T(8,128)(2,1)} custom-call(s32[16]{0:T(128)} %partner_ref.1, bf16[128,32,128]{2,1,0:T(8,128)(2,1)} %copy.5.rows_ref, bf16[8,128,256]{2,1,0:T(8,128)(2,1)} %constant.20.clone.lag_ref), custom_call_target="tpu_custom_call" | custom-call | tf_op jit(solution)/shard_map/pairs/pallas_call | solution.py:456
  172.8 4.7 %copy.7 = bf16[32,512,128]{2,1,0:T(8,128)(2,1)} copy(bf16[32,512,128]{2,1,0:T(8,128)(2,1)} %pairs.1) | data formatting | bytes 8388608
  (2 shorter events, 0.0 us)
Async XLA Ops:
  0.0 2.5 %copy-start = (bf16[32,8,2048]{2,1,0:T(8,128)(2,1)S(1)}, bf16[32,8,2048]{2,1,0:T(8,128)(2,1)}, u32[]{:S(2)}) copy-start(bf16[32,8,2048]{2,1,0:T(8,128)(2,1)} %param.3) | copy-start | bytes 3145732

commit v4 on v3

--- a/solution.py
+++ b/solution.py
@@ -19,9 +19,10 @@
 INNER = 8
 CHUNK = 16
 STEPS = COLS // CHUNK
+TILES = ((0, 256), (256, 128), (384, 128))
 TILE = 256
-GROUP_COLS = 4
-GROUP_CH = 8
+GROUP_COLS = 8
+GROUP_CH = 16
 AXES = ("x", "yh", "core", "ylo", "z")
 MESH = pl.DeviceIdType.MESH
 
@@ -118,20 +119,12 @@
     own_share = pltpu.make_async_copy(
         rows_ref.at[pl.ds(pl.multiple_of(group * 8, 8), 8)], spread.at[group], local_sem.at[0]
     )
-    own_swap = pltpu.make_async_remote_copy(
-        src_ref=rows_ref, dst_ref=own, send_sem=own_send, recv_sem=own_recv,
-        device_id=mirror, device_id_type=MESH,
-    )
     own_stay = pltpu.make_async_copy(rows_ref, own, local_sem.at[1])
 
     own_share.start()
     for t in range(1, 16):
         share(t).start()
 
-    @pl.when(moved)
-    def _():
-        own_swap.start()
-
     @pl.when(jnp.logical_not(moved))
     def _():
         own_stay.start()
@@ -150,6 +143,13 @@
     def place(c, dist, member):
         start = SLOT[dist] * 64 + member * 32
         return gathered.at[columns(c), pl.ds(pl.multiple_of(start, 32), 32), :]
+
+    def own_swap(c):
+        return pltpu.make_async_remote_copy(
+            src_ref=rows_ref.at[columns(c)], dst_ref=own.at[columns(c)],
+            send_sem=own_send.at[c], recv_sem=own_recv.at[c],
+            device_id=mirror, device_id_type=MESH,
+        )
 
     def share_place(source, member):
         cols = pl.ds(pl.multiple_of(source * 8, 8), 8)
@@ -197,6 +197,11 @@
         for member in range(2):
             give(t, member).start()
 
+    @pl.when(moved)
+    def _():
+        for c in range(STEPS):
+            own_swap(c).start()
+
     def wait_part(c):
         for source_core in range(2):
             stays = jnp.logical_and(
@@ -243,12 +248,13 @@
         )
 
     def result_pieces(tile):
-        for piece in range(4):
-            from_z = lax.rem(z + DIST[tile * 4 + piece] + 8, 8)
+        first, width = TILES[tile]
+        for slot in range(first // 64, (first + width) // 64):
+            from_z = lax.rem(z + DIST[slot] + 8, 8)
             for member in range(2):
-                rows = pl.ds(piece * 64 + member * 32, 32)
+                rows = pl.ds(slot * 64 + member * 32, 32)
                 target = pl.ds(pl.multiple_of((member * 8 + from_z) * 32, 32), 32)
-                yield tile * 8 + piece * 2 + member, result.at[tile, :, rows, :], target
+                yield slot * 2 + member, result.at[:, rows, :], target
 
     def result_remote(index, src, target):
         return pltpu.make_async_remote_copy(
@@ -282,6 +288,7 @@
         xs_rows[column] = pltpu.roll(value, 64, 1) * sign
 
     def cross_column(c, i, lane_slot, tile):
+        first, width = TILES[tile]
         column = lax.rem(c + chip, STEPS) * CHUNK + i
         for a in range(CH):
             re_row = jnp.broadcast_to(x_rows[column, pl.ds(a, 1), :], (INNER, COLS))
@@ -290,19 +297,27 @@
                 [jnp.where(mask, re_row, 0.0), jnp.where(mask, im_row, 0.0)], axis=0
             )
             left[lane_slot, pl.ds(a * 16, 16), :] = block.astype(jnp.bfloat16)
-        right = gathered[column, pl.ds(pl.multiple_of(tile * TILE, TILE), TILE), :]
+        right = gathered[column, first : first + width, :]
         product = lax.dot_general(
             left[lane_slot], right, (((1,), (1,)), ((), ())), preferred_element_type=jnp.float32
         )
-        cross[:, pl.ds(pl.multiple_of(i * 16, 16), 16), :] = product.astype(
+        cross[:, pl.ds(pl.multiple_of(i * 16, 16), 16), :width] = product.astype(
             jnp.bfloat16
-        ).reshape(CH, 16, TILE)
-
-    def lag_channel(c, a):
-        product = jnp.dot(lag_ref[lax.rem(c + chip, STEPS)], cross[a], preferred_element_type=jnp.float32)
-        total[a] = jnp.where(c > 0, total[a], 0.0) + product
+        ).reshape(CH, 16, width)
+
+    def lag_channel(c, a, tile):
+        first, width = TILES[tile]
+        lanes = slice(first, first + width)
+        product = jnp.dot(
+            lag_ref[lax.rem(c + chip, STEPS)], cross[a, :, :width],
+            preferred_element_type=jnp.float32,
+        )
+        total[a, :, lanes] = jnp.where(c > 0, total[a, :, lanes], 0.0) + product
 
     def compute(c, tile):
+        first, width = TILES[tile]
+        lanes = slice(first, first + width)
+
         @pl.loop(0, CHUNK // GROUP_COLS)
         def _(i):
             for u in range(GROUP_COLS):
@@ -311,14 +326,17 @@
         @pl.loop(0, CH // GROUP_CH)
         def _(i):
             for u in range(GROUP_CH):
-                lag_channel(c, i * GROUP_CH + u)
+                lag_channel(c, i * GROUP_CH + u, tile)
 
         @pl.when(c == STEPS - 1)
         def _():
             @pl.loop(0, CH // 4)
             def _(i):
                 for u in range(4):
-                    result[tile, i * 4 + u] = total[i * 4 + u].T.astype(jnp.bfloat16)
+                    a = i * 4 + u
+                    result[a, lanes, :] = total[a, :, lanes].T.astype(jnp.bfloat16)
+
+            send_result(tile)
 
     def inside(c):
         return jnp.logical_and(c >= 0, c < STEPS)
@@ -353,17 +371,23 @@
             hop(c, -1, -1).wait_recv()
             across(c, -2).start()
 
-        @pl.when(inside(t - 3))
-        def _():
-            c = t - 3
+        @pl.when(inside(t - 1))
+        def _():
+            c = t - 1
             hop(c, 2, 1).start()
             hop(c, -2, -1).start()
 
-        @pl.when(inside(t - 5))
-        def _():
-            c = t - 5
+        @pl.when(inside(t - 3))
+        def _():
+            c = t - 3
             hop(c, 2, 1).wait_recv()
             hop(c, -2, -1).wait_recv()
+            across(c, 3).start()
+            across(c, -3).start()
+
+        @pl.when(inside(t - 5))
+        def _():
+            c = t - 5
 
             @pl.when(lax.rem(c, 2) == 0)
             def _():
@@ -373,55 +397,50 @@
             def _():
                 hop(c, -3, -1).start()
 
-            across(c, 3).start()
-            across(c, -3).start()
-
         @pl.when(inside(t - 7))
         def _():
             c = t - 7
             hop(c, 3, 1).wait_recv()
             across(c, 4).start()
 
-        @pl.when(t == -3)
+        @pl.when(jnp.logical_and(t == 0, jnp.logical_not(moved)))
+        def _():
+            own_stay.wait()
+
+        @pl.when(inside(t))
         def _():
             @pl.when(moved)
             def _():
-                own_swap.wait_recv()
-
-            @pl.when(jnp.logical_not(moved))
-            def _():
-                own_stay.wait()
-
-        @pl.when(jnp.logical_and(t >= -3, t < 0))
-        def _():
-            @pl.loop(0, 43)
+                own_swap(t).wait_recv()
+
+            @pl.loop(0, CHUNK // 4)
             def _(i):
-                load_rows(jnp.minimum((t + 3) * 43 + i, COLS - 1))
-
-        @pl.when(inside(t))
-        def _():
+                for u in range(4):
+                    load_rows(lax.rem(t + chip, STEPS) * CHUNK + i * 4 + u)
+
             for dist in (0, 1, -1, 2):
                 across_in(t, dist).wait_recv()
             compute(t, 0)
 
-        @pl.when(t == STEPS)
-        def _():
-            send_result(0)
-
-        @pl.when(t >= STEPS)
-        def _():
-            for dist in (-2, 3, -3, 4):
-                across_in(t - STEPS, dist).wait_recv()
-            compute(t - STEPS, 1)
-
-    send_result(1)
+        @pl.when(inside(t - 4))
+        def _():
+            for dist in (-2, 3):
+                across_in(t - 4, dist).wait_recv()
+            compute(t - 4, 1)
+
+        @pl.when(inside(t - 8))
+        def _():
+            for dist in (-3, 4):
+                across_in(t - 8, dist).wait_recv()
+            compute(t - 8, 2)
 
     for t in range(1, 16):
         share(t).wait_send()
 
     @pl.when(moved)
     def _():
-        own_swap.wait_send()
+        for c in range(STEPS):
+            own_swap(c).wait_send()
 
     for member in range(2):
         @pl.when(jnp.logical_or(moved, ylo != member))
@@ -441,13 +460,13 @@
 
     @pl.when(moved)
     def _():
-        for tile in range(2):
+        for tile in range(len(TILES)):
             for piece in result_pieces(tile):
                 result_remote(*piece).wait()
 
     @pl.when(jnp.logical_not(moved))
     def _():
-        for tile in range(2):
+        for tile in range(len(TILES)):
             for piece in result_pieces(tile):
                 result_local(*piece).wait()
 
@@ -471,13 +490,13 @@
             pltpu.VMEM((COLS, 16 * CH, COLS), jnp.bfloat16),
             pltpu.VMEM((GROUP_COLS, CH * 16, COLS), jnp.bfloat16),
             pltpu.VMEM((CH, TILE, TILE), jnp.bfloat16),
-            pltpu.VMEM((CH, LAGS, TILE), jnp.float32),
-            pltpu.VMEM((2, CH, TILE, LAGS), jnp.bfloat16),
+            pltpu.VMEM((CH, LAGS, 16 * CH), jnp.float32),
+            pltpu.VMEM((CH, 16 * CH, LAGS), jnp.bfloat16),
             pltpu.SemaphoreType.DMA((3,)),
             pltpu.SemaphoreType.DMA((16,)),
             pltpu.SemaphoreType.DMA((16,)),
-            pltpu.SemaphoreType.DMA,
-            pltpu.SemaphoreType.DMA,
+            pltpu.SemaphoreType.DMA((STEPS,)),
+            pltpu.SemaphoreType.DMA((STEPS,)),
             pltpu.SemaphoreType.DMA((16,)),
             pltpu.SemaphoreType.DMA((16,)),
             pltpu.SemaphoreType.DMA((STEPS, 2, 8)),

time: 178 us -> 169 us (0.949)
  Pallas kernels: 168 us -> 160 us
    pallas_call x1, Pallas kernels: 168 us -> 160 us  [correlate_pairs(): pl.pallas_call(pair_kernel, out_shape=jax.ShapeDtypeStruct((CH, 16 * CH,...]
where the time goes in v4:
time: 169 us
  Pallas kernels  160 us (95%)
  local copies, waits for them, and re-layouts  6.33 us (4%)
  other arithmetic  2.05 us (1%)
    pallas_call x1, Pallas kernels, correlate_pairs(): pl.pallas_call(pair_kernel, out_shape=jax.ShapeDtypeStruct((CH, 16 * CH,...  160 us
    unnamed x3, local copies, waits for them, and re-layouts  4.66 us

profile of v4, /device:TPU:1, one launch (start us, length us, event | category | flops | bytes accessed | tf_op | source)
XLA Modules:
  0.0 169.0 jit_solution(12165431207180395260)
XLA Ops:
  0.0 0.0 copy-start
  0.0 1.7 %add_reduce_fusion = f32[32,1024]{1,0:T(8,128)S(1)} fusion(bf16[32,8,2048]{2,1,0:T(8,128)(2,1)} %param.3), kind=kLoop, calls=%fused_computation.8 | loop fusion | flops 1540096 | bytes 1179648 | tf_op jit(solution)/shard_map/reduce_sum | solution.py:46
  1.7 0.7 fusion.4
  2.5 0.0 copy-done
  2.5 0.3 fusion.5
  2.8 1.7 copy.5.rows_ref
  4.5 159.9 %pairs.1 = bf16[32,512,128]{2,1,0:T(8,128)(2,1)} custom-call(s32[16]{0:T(128)} %partner_ref.1, bf16[128,32,128]{2,1,0:T(8,128)(2,1)} %copy.5.rows_ref, bf16[8,128,256]{2,1,0:T(8,128)(2,1)} %constant.20.clone.lag_ref), custom_call_target="tpu_custom_call" | custom-call | tf_op jit(solution)/shard_map/pairs/pallas_call | solution.py:475
  164.4 4.7 %copy.7 = bf16[32,512,128]{2,1,0:T(8,128)(2,1)} copy(bf16[32,512,128]{2,1,0:T(8,128)(2,1)} %pairs.1) | data formatting | bytes 8388608
  (2 shorter events, 0.0 us)
Async XLA Ops:
  0.0 2.5 %copy-start = (bf16[32,8,2048]{2,1,0:T(8,128)(2,1)S(1)}, bf16[32,8,2048]{2,1,0:T(8,128)(2,1)}, u32[]{:S(2)}) copy-start(bf16[32,8,2048]{2,1,0:T(8,128)(2,1)} %param.3) | copy-start | bytes 3145732

commit v5 on v4

--- a/solution.py
+++ b/solution.py
@@ -341,13 +341,42 @@
     def inside(c):
         return jnp.logical_and(c >= 0, c < STEPS)
 
-    @pl.loop(0, 2 * STEPS + 5)
+    def start_third(c):
+        @pl.when(inside(c))
+        def _():
+            hop(c, 2, 1).start()
+            hop(c, -2, -1).start()
+
+    def end_third(c):
+        @pl.when(inside(c))
+        def _():
+            hop(c, 2, 1).wait_recv()
+            across(c, 3).start()
+            hop(c, -2, -1).wait_recv()
+            across(c, -3).start()
+
+    def middle_tile(c):
+        @pl.when(inside(c))
+        def _():
+            for dist in (-2, 3):
+                across_in(c, dist).wait_recv()
+            compute(c, 1)
+
+    @pl.loop(0, 18)
     def _(tick):
-        t = tick - 5
+        t = tick - 3
 
         @pl.when(inside(t + 3))
         def _():
             c = t + 3
+            wait_part(c)
+            hop(c, 0, 1).start()
+            hop(c, 0, -1).start()
+            across(c, 0).start()
+
+        @pl.when(inside(t + 2))
+        def _():
+            c = t + 2
             hop(c, 0, 1).wait_recv()
             hop(c, 1, 1).start()
             hop(c, 0, -1).wait_recv()
@@ -355,14 +384,6 @@
             across(c, 1).start()
             across(c, -1).start()
 
-        @pl.when(inside(t + 5))
-        def _():
-            c = t + 5
-            wait_part(c)
-            hop(c, 0, 1).start()
-            hop(c, 0, -1).start()
-            across(c, 0).start()
-
         @pl.when(inside(t + 1))
         def _():
             c = t + 1
@@ -371,37 +392,22 @@
             hop(c, -1, -1).wait_recv()
             across(c, -2).start()
 
-        @pl.when(inside(t - 1))
-        def _():
-            c = t - 1
-            hop(c, 2, 1).start()
-            hop(c, -2, -1).start()
-
-        @pl.when(inside(t - 3))
-        def _():
-            c = t - 3
-            hop(c, 2, 1).wait_recv()
-            hop(c, -2, -1).wait_recv()
-            across(c, 3).start()
-            across(c, -3).start()
-
-        @pl.when(inside(t - 5))
-        def _():
-            c = t - 5
-
-            @pl.when(lax.rem(c, 2) == 0)
-            def _():
-                hop(c, 3, 1).start()
-
-            @pl.when(lax.rem(c, 2) == 1)
-            def _():
-                hop(c, -3, -1).start()
-
-        @pl.when(inside(t - 7))
-        def _():
-            c = t - 7
-            hop(c, 3, 1).wait_recv()
-            across(c, 4).start()
+        start_third(2 * t - 11)
+        start_third(2 * t - 10)
+
+        @pl.when(inside(2 * t - 18))
+        def _():
+            hop(2 * t - 18, 3, 1).start()
+            hop(2 * t - 17, -3, -1).start()
+
+        end_third(2 * t - 13)
+        end_third(2 * t - 12)
+
+        @pl.when(inside(2 * t - 20))
+        def _():
+            for c in (2 * t - 20, 2 * t - 19):
+                hop(c, 3, 1).wait_recv()
+                across(c, 4).start()
 
         @pl.when(jnp.logical_and(t == 0, jnp.logical_not(moved)))
         def _():
@@ -422,17 +428,19 @@
                 across_in(t, dist).wait_recv()
             compute(t, 0)
 
-        @pl.when(inside(t - 4))
-        def _():
-            for dist in (-2, 3):
-                across_in(t - 4, dist).wait_recv()
-            compute(t - 4, 1)
-
-        @pl.when(inside(t - 8))
-        def _():
-            for dist in (-3, 4):
-                across_in(t - 8, dist).wait_recv()
-            compute(t - 8, 2)
+        @pl.loop(0, 2)
+        def _(k):
+            middle_tile(2 * t - 15 + k)
+
+        @pl.loop(0, 2)
+        def _(k):
+            c = 2 * t - 22 + k
+
+            @pl.when(inside(c))
+            def _():
+                for dist in (-3, 4):
+                    across_in(c, dist).wait_recv()
+                compute(c, 2)
 
     for t in range(1, 16):
         share(t).wait_send()

time: 169 us -> 169 us (level)
  no operation moved by 1% of the time
where the time goes in v5:
time: 169 us
  Pallas kernels  160 us (95%)
  local copies, waits for them, and re-layouts  6.33 us (4%)
  other arithmetic  2.05 us (1%)
    pallas_call x1, Pallas kernels, correlate_pairs(): pl.pallas_call(pair_kernel, out_shape=jax.ShapeDtypeStruct((CH, 16 * CH,...  160 us
    unnamed x3, local copies, waits for them, and re-layouts  4.66 us

profile of v5, /device:TPU:1, one launch (start us, length us, event | category | flops | bytes accessed | tf_op | source)
XLA Modules:
  0.0 169.3 jit_solution(8334149625269876811)
XLA Ops:
  0.0 0.0 copy-start
  0.0 1.7 %add_reduce_fusion = f32[32,1024]{1,0:T(8,128)S(1)} fusion(bf16[32,8,2048]{2,1,0:T(8,128)(2,1)} %param.3), kind=kLoop, calls=%fused_computation.8 | loop fusion | flops 1540096 | bytes 1179648 | tf_op jit(solution)/shard_map/reduce_sum | solution.py:46
  1.7 0.7 fusion.4
  2.5 0.0 copy-done
  2.5 0.3 fusion.5
  2.8 1.7 copy.5.rows_ref
  4.5 160.1 %pairs.1 = bf16[32,512,128]{2,1,0:T(8,128)(2,1)} custom-call(s32[16]{0:T(128)} %partner_ref.1, bf16[128,32,128]{2,1,0:T(8,128)(2,1)} %copy.5.rows_ref, bf16[8,128,256]{2,1,0:T(8,128)(2,1)} %constant.20.clone.lag_ref), custom_call_target="tpu_custom_call" | custom-call | tf_op jit(solution)/shard_map/pairs/pallas_call | solution.py:483
  164.6 4.7 %copy.7 = bf16[32,512,128]{2,1,0:T(8,128)(2,1)} copy(bf16[32,512,128]{2,1,0:T(8,128)(2,1)} %pairs.1) | data formatting | bytes 8388608
  (2 shorter events, 0.0 us)
Async XLA Ops:
  0.0 2.5 %copy-start = (bf16[32,8,2048]{2,1,0:T(8,128)(2,1)S(1)}, bf16[32,8,2048]{2,1,0:T(8,128)(2,1)}, u32[]{:S(2)}) copy-start(bf16[32,8,2048]{2,1,0:T(8,128)(2,1)} %param.3) | copy-start | bytes 3145732

commit v6 on v5

--- a/solution.py
+++ b/solution.py
@@ -65,7 +65,7 @@
 
 def pair_kernel(
     partner_ref, rows_ref, lag_ref, out_ref,
-    spread, ordered, own, x_rows, xs_rows, gathered, left, cross, total, result,
+    spread, ordered, own, x_rows, xs_rows, gathered, left, left_pair, cross, total, result,
     local_sem, spread_send, spread_recv, own_send, own_recv, part_send, part_recv,
     recv_sem, send_sem, out_send, out_recv,
 ):
@@ -305,6 +305,51 @@
             jnp.bfloat16
         ).reshape(CH, 16, width)
 
+    def cross_pair(c, i, pair_slot, tile):
+        first, width = TILES[tile]
+        column = lax.rem(c + chip, STEPS) * CHUNK + i
+        for half in range(2):
+            for a in range(CH):
+                re_row = jnp.broadcast_to(x_rows[column + half, pl.ds(a, 1), :], (INNER, COLS))
+                im_row = jnp.broadcast_to(xs_rows[column + half, pl.ds(a, 1), :], (INNER, COLS))
+                block = jnp.concatenate(
+                    [jnp.where(mask, re_row, 0.0), jnp.where(mask, im_row, 0.0)], axis=0
+                )
+                left_pair[
+                    pair_slot, pl.ds(a * 16, 16), half * COLS : (half + 1) * COLS
+                ] = block.astype(jnp.bfloat16)
+        none = jnp.zeros((width, COLS), jnp.bfloat16)
+        right = jnp.concatenate(
+            [
+                jnp.concatenate([gathered[column, first : first + width, :], none], axis=1),
+                jnp.concatenate([none, gathered[column + 1, first : first + width, :]], axis=1),
+            ],
+            axis=0,
+        )
+        product = lax.dot_general(
+            left_pair[pair_slot], right, (((1,), (1,)), ((), ())),
+            preferred_element_type=jnp.float32,
+        )
+        product = product.astype(jnp.bfloat16).reshape(CH // 2, 2, 16, 2 * width)
+        for half in range(2):
+            rows = pl.ds(pl.multiple_of((i + half) * 16, 16), 16)
+            lanes = slice(half * width, (half + 1) * width)
+            for odd in range(2):
+                cross[: CH // 2, rows, odd * width : (odd + 1) * width] = product[:, odd, :, lanes]
+
+    def lag_pair(c, pair, tile):
+        first, width = TILES[tile]
+        lanes = slice(first, first + width)
+        product = jnp.dot(
+            lag_ref[lax.rem(c + chip, STEPS)], cross[pair], preferred_element_type=jnp.float32
+        )
+        for odd in range(2):
+            a = pair * 2 + odd
+            total[a, :, lanes] = (
+                jnp.where(c > 0, total[a, :, lanes], 0.0)
+                + product[:, odd * width : (odd + 1) * width]
+            )
+
     def lag_channel(c, a, tile):
         first, width = TILES[tile]
         lanes = slice(first, first + width)
@@ -318,15 +363,27 @@
         first, width = TILES[tile]
         lanes = slice(first, first + width)
 
-        @pl.loop(0, CHUNK // GROUP_COLS)
-        def _(i):
-            for u in range(GROUP_COLS):
-                cross_column(c, i * GROUP_COLS + u, u, tile)
-
-        @pl.loop(0, CH // GROUP_CH)
-        def _(i):
-            for u in range(GROUP_CH):
-                lag_channel(c, i * GROUP_CH + u, tile)
+        if width == TILE:
+
+            @pl.loop(0, CHUNK // GROUP_COLS)
+            def _(i):
+                for u in range(GROUP_COLS):
+                    cross_column(c, i * GROUP_COLS + u, u, tile)
+
+            @pl.loop(0, CH // GROUP_CH)
+            def _(i):
+                for u in range(GROUP_CH):
+                    lag_channel(c, i * GROUP_CH + u, tile)
+
+        else:
+
+            @pl.loop(0, CHUNK // GROUP_COLS)
+            def _(i):
+                for u in range(GROUP_COLS // 2):
+                    cross_pair(c, i * GROUP_COLS + u * 2, u, tile)
+
+            for pair in range(CH // 2):
+                lag_pair(c, pair, tile)
 
         @pl.when(c == STEPS - 1)
         def _():
@@ -497,6 +554,7 @@
             pltpu.VMEM((COLS, CH, COLS), jnp.float32),
             pltpu.VMEM((COLS, 16 * CH, COLS), jnp.bfloat16),
             pltpu.VMEM((GROUP_COLS, CH * 16, COLS), jnp.bfloat16),
+            pltpu.VMEM((GROUP_COLS // 2, CH * 16, 2 * COLS), jnp.bfloat16),
             pltpu.VMEM((CH, TILE, TILE), jnp.bfloat16),
             pltpu.VMEM((CH, LAGS, 16 * CH), jnp.float32),
             pltpu.VMEM((CH, 16 * CH, LAGS), jnp.bfloat16),

time: 169 us -> 167 us (0.988)
  Pallas kernels: 160 us -> 158 us
    pallas_call x1, Pallas kernels: 160 us -> 158 us  [correlate_pairs(): pl.pallas_call(pair_kernel, out_shape=jax.ShapeDtypeStruct((CH, 16 * CH,...]
where the time goes in v6:
time: 167 us
  Pallas kernels  158 us (95%)
  local copies, waits for them, and re-layouts  6.33 us (4%)
  other arithmetic  2.05 us (1%)
    pallas_call x1, Pallas kernels, correlate_pairs(): pl.pallas_call(pair_kernel, out_shape=jax.ShapeDtypeStruct((CH, 16 * CH,...  158 us
    unnamed x3, local copies, waits for them, and re-layouts  4.66 us

profile of v6, /device:TPU:1, one launch (start us, length us, event | category | flops | bytes accessed | tf_op | source)
XLA Modules:
  0.0 167.1 jit_solution(4297003562337953144)
XLA Ops:
  0.0 0.0 copy-start
  0.0 1.7 %add_reduce_fusion = f32[32,1024]{1,0:T(8,128)S(1)} fusion(bf16[32,8,2048]{2,1,0:T(8,128)(2,1)} %param.3), kind=kLoop, calls=%fused_computation.8 | loop fusion | flops 1540096 | bytes 1179648 | tf_op jit(solution)/shard_map/reduce_sum | solution.py:46
  1.7 0.7 fusion.4
  2.5 0.0 copy-done
  2.5 0.3 fusion.5
  2.8 1.7 %copy.5.rows_ref = bf16[128,32,128]{2,1,0:T(8,128)(2,1)} copy(bf16[128,32,128]{0,2,1:T(8,128)(2,1)S(1)} %fusion.5) | data formatting | bytes 2097152 | tf_op jit(solution)/shard_map/reshape | solution.py:583
  4.5 157.9 %pairs.1 = bf16[32,512,128]{2,1,0:T(8,128)(2,1)} custom-call(s32[16]{0:T(128)} %partner_ref.1, bf16[128,32,128]{2,1,0:T(8,128)(2,1)} %copy.5.rows_ref, bf16[8,128,256]{2,1,0:T(8,128)(2,1)} %constant.20.clone.lag_ref), custom_call_target="tpu_custom_call" | custom-call | tf_op jit(solution)/shard_map/pairs/pallas_call | solution.py:540
  162.5 4.7 %copy.7 = bf16[32,512,128]{2,1,0:T(8,128)(2,1)} copy(bf16[32,512,128]{2,1,0:T(8,128)(2,1)} %pairs.1) | data formatting | bytes 8388608
  (2 shorter events, 0.0 us)
Async XLA Ops:
  0.0 2.5 %copy-start = (bf16[32,8,2048]{2,1,0:T(8,128)(2,1)S(1)}, bf16[32,8,2048]{2,1,0:T(8,128)(2,1)}, u32[]{:S(2)}) copy-start(bf16[32,8,2048]{2,1,0:T(8,128)(2,1)} %param.3) | copy-start | bytes 3145732
